TPU v7x, 512 devices: a whole 4x8x8 slice. The times are simulated.
512 devices in a mesh: leaf: 8 (over y), grow: 8 (over z), gcol: 8 (over x, core).
Axes of the slice: x: 4, y: 8, z: 8, core: 2. Of those that a mesh axis runs over, the one named last changes fastest.
Arguments:
- right_leaf: float32 [8, 8, 8, 512, 256], P('leaf', 'grow', 'gcol'), may hold values from -6 to 6
- inverse_leaf: float32 [8, 8, 8, 512, 512], P('leaf', 'grow', 'gcol'), may hold values from -2 to 2
- lower_leaf: float32 [8, 8, 8, 512, 512], P('leaf', 'grow', 'gcol'), may hold values from -0.25 to 0.25
- present: int32 [8, 8, 8], P('leaf', 'grow', 'gcol'), may hold values 0 or 1
- right_middle: float32 [8, 8, 512, 256], P('leaf', 'grow', 'gcol'), may hold values from -6 to 6
- inverse_middle: float32 [8, 8, 512, 512], P('leaf', 'grow', 'gcol'), may hold values from -2 to 2
- upper_middle: float32 [2, 8, 8, 512, 512], P(None, 'leaf', 'grow', 'gcol'), may hold values from -0.03125 to 0.03125
- right_top: float32 [2, 512, 256], P(None, 'gcol'), may hold values from -6 to 6
- inverse_top: float32 [2, 512, 512], P(None, 'gcol'), may hold values from -2 to 2
- upper_top: float32 [1, 512, 512], P(None, 'gcol'), may hold values from -0.25 to 0.25
Outputs:
- solve_leaf: float32 [8, 8, 8, 512, 256], P('leaf', 'grow', 'gcol')
- solve_middle: float32 [8, 8, 512, 256], P('leaf', 'grow', 'gcol')
- solve_top: float32 [2, 512, 256], P(None, 'gcol')
All inputs are finite; a program needn't handle non-finite values. No bound on the sum of `present` on one device may be relied on, other than what follows from the above.
Results may differ from a plain program's by a relative error of at most 0.00016.
Values sent between devices are 32-bit elements; how exact they have to be, the bound alone decides.
No kernel may reach another device: no remote copies, remote signals or barrier semaphores. Data moves between devices by JAX's collectives and lax.ppermute only.
A program may use at most 64 MiB of HBM per device.

v0:
```python
import jax
import jax.numpy as jnp
from jax import lax
from jax.sharding import Mesh
from jax.sharding import PartitionSpec as P

GROW_GCOL = ("grow", "gcol_0", "gcol_1")
GCOL = ("gcol_0", "gcol_1")


PRECISE = lax.Precision.HIGHEST


def by_axis(x, axes):
    for axis in axes:
        x = lax.psum(x, axis)
    return x


def from_partner(value, axis, apart):
    mask = 2**apart
    pairs = [(source, source ^ mask) for source in range(lax.axis_size(axis))]
    return lax.ppermute(value, axis, pairs)


def gather_turned(arrays, axis, dims):
    turned = [jnp.moveaxis(a, dim, 0) for a, dim in zip(arrays, dims)]
    both = jnp.concatenate([t.reshape(len(t), -1) for t in turned], axis=1)
    filled, at, finished = (lax.all_gather(both, axis, axis=0, tiled=True), 0, [])
    for t, dim in zip(turned, dims):
        piece = filled[:, at : at + t[0].size].reshape(-1, *t.shape[1:])
        finished.append(jnp.moveaxis(piece, 0, dim))
        at += t[0].size
    return tuple(finished)


def from_everyone(x, axis):
    copies = jnp.broadcast_to(x, (lax.axis_size(axis), *x.shape))
    return lax.all_to_all(copies, axis, split_axis=0, concat_axis=0, tiled=True)


def over_copies(x, axis):
    everything = from_everyone(x, axis)
    return jnp.sum(everything, axis=0)


def product(factor, vector):
    return jnp.dot(factor, vector, precision=PRECISE, preferred_element_type=jnp.float32)


def transposed_product(factor, vector):
    return lax.dot_general(
        factor,
        vector,
        (((0,), (0,)), ((), ())),
        precision=PRECISE,
        preferred_element_type=jnp.float32,
    )


def pair_index(upper_level, lower_level):
    return upper_level * (upper_level - 1) // 2 + lower_level


def widen(fragment, row_start, full_rows):
    blank = jnp.zeros((full_rows, fragment.shape[1]), jnp.float32)
    return lax.dynamic_update_slice_in_dim(blank, fragment, row_start, 0)


def combine_layers(stacked, row_keep):
    stacked = by_axis(stacked * row_keep, GROW_GCOL)
    for which_bit in range(lax.axis_size("leaf").bit_length() - 1):
        partner = from_partner(stacked, "leaf", which_bit)
        stacked = stacked + partner
    return stacked


def local(
    right_leaf,
    inverse_leaf,
    lower_leaf,
    present,
    right_middle,
    inverse_middle,
    upper_middle,
    right_top,
    inverse_top,
    upper_top,
):
    levels_count = right_top.shape[0]
    block_size = inverse_leaf.shape[-1]
    share_rows = inverse_middle.shape[2]
    row_start = lax.axis_index(GCOL) * share_rows
    inverse_middle, upper_middle, inverse_top, upper_top = gather_turned(
        (inverse_middle, upper_middle, inverse_top, upper_top), GCOL, (2, 3, 1, 1)
    )
    row_ids = lax.broadcasted_iota(jnp.int32, (1, block_size, 1), 1)
    row_keep = ((row_ids >= row_start) & (row_ids < row_start + share_rows)).astype(jnp.float32)
    kept_block = present[0, 0, 0].astype(jnp.float32)
    leaf_fwd = product(inverse_leaf[0, 0, 0], right_leaf[0, 0, 0])
    middle_part = product(lower_leaf[0, 0, 0], leaf_fwd * kept_block) - widen(
        right_middle[0, 0], row_start, block_size
    )
    middle_total = over_copies(middle_part, GCOL)
    middle_fwd = product(inverse_middle[0, 0], -middle_total)
    lead_device = jnp.where(
        (lax.axis_index("leaf") == 0) & (lax.axis_index("grow") == 0), 1.0, 0.0
    ).astype(jnp.float32)
    top_rights = [widen(right_top[height], row_start, block_size) for height in range(levels_count)]
    partials = [
        transposed_product(upper_middle[height, 0, 0], middle_fwd)
        - lead_device * top_rights[height] * row_keep[0]
        for height in range(levels_count)
    ]
    top_fwd = []
    totals = combine_layers(jnp.stack(partials), row_keep)
    for upper_level in range(levels_count):
        residual = -totals[upper_level]
        if upper_level > 0:
            link_terms = transposed_product(upper_top[pair_index(upper_level, 0)], top_fwd[0])
            residual = residual - link_terms
        top_fwd.append(product(inverse_top[upper_level], residual))
    top_back = [None] * levels_count
    for upper_level in reversed(range(levels_count)):
        residual = top_fwd[upper_level]
        for higher_level in range(upper_level + 1, levels_count):
            residual = residual - product(
                upper_top[pair_index(higher_level, upper_level)], top_back[higher_level]
            )
        top_piece = transposed_product(inverse_top[upper_level], residual)
        top_back[upper_level] = top_piece
    middle_res = middle_fwd
    for height in range(levels_count):
        middle_res = middle_res - product(upper_middle[height, 0, 0], top_back[height])
    middle_piece = transposed_product(inverse_middle[0, 0], middle_res)
    leaf_res = leaf_fwd - transposed_product(lower_leaf[0, 0, 0], middle_piece) * kept_block
    leaf_back = transposed_product(inverse_leaf[0, 0, 0], leaf_res)
    solve_middle = lax.dynamic_slice_in_dim(middle_piece, row_start, share_rows, 0)
    solve_top = jnp.stack(
        [lax.dynamic_slice_in_dim(top_whole, row_start, share_rows, 0) for top_whole in top_back]
    )
    return (leaf_back[None, None, None], solve_middle[None, None], solve_top)


def solution(mesh):
    split = Mesh(
        mesh.devices.reshape(mesh.shape["leaf"], mesh.shape["grow"], 4, 2),
        ("leaf", "grow", "gcol_0", "gcol_1"),
    )
    in_specs = (
        P("leaf", "grow", GCOL, None, None),
        P("leaf", "grow", GCOL, None, None),
        P("leaf", "grow", GCOL, None, None),
        P("leaf", "grow", GCOL),
        P("leaf", "grow", GCOL, None),
        P("leaf", "grow", GCOL, None),
        P(None, "leaf", "grow", GCOL, None),
        P(None, GCOL, None),
        P(None, GCOL, None),
        P(None, GCOL, None),
    )
    out_specs = (
        P("leaf", "grow", GCOL, None, None),
        P("leaf", "grow", GCOL, None),
        P(None, GCOL, None),
    )
    return jax.shard_map(local, mesh=split, in_specs=in_specs, out_specs=out_specs, check_vma=False)
```

profile of v0, /device:TPU:1, one launch (start us, length us, event | category | flops | bytes accessed | tf_op | source)
XLA Modules:
  0.0 463.2 jit_solution(894214524301879882)
XLA Ops:
  7.2 0.0 copy-start
  7.2 0.0 all-gather.2.cloned.1.call-start
  7.2 1.2 copy.17
  8.5 1.0 copy.38
  9.5 1.9 pad_maximum_fusion
  11.4 0.0 all-gather.2.cloned.1.call-update
  11.4 0.9 copy.19
  13.0 0.1 broadcast.23.clone
  13.1 1.3 dynamic_update_slice.9
  14.4 2.3 fusion.20
  16.8 0.8 copy-done.7
  17.6 1.9 fusion.4
  19.5 0.2 copy.20
  19.7 2.4 broadcast_in_dim.9
  22.1 11.0 %all-to-all-start = ((f32[8,512,256]{2,1,0:T(8,128)}), f32[8,512,256]{2,1,0:T(8,128)}, u32[]{:S(2)}, u32[]{:S(2)}) async-start(f32[8,512,256]{2,1,0:T(8,128)} %broadcast_in_dim.9), calls=%async_computation | async-start | bytes 8388608 | tf_op jit(solution)/shard_map/all_to_all | solution.py:39
  33.2 0.1 copy.37
  33.3 0.1 copy.36
  33.4 0.1 broadcast.23.clone.1
  33.4 1.3 dynamic_update_slice.11
  34.8 0.8 copy-done.12
  35.6 1.3 dynamic_update_slice.10
  37.0 69.9 %all-to-all-done = f32[8,512,256]{2,1,0:T(8,128)} async-done(((f32[8,512,256]{2,1,0:T(8,128)}), f32[8,512,256]{2,1,0:T(8,128)}, u32[]{:S(2)}, u32[]{:S(2)}) %all-to-all-start) | async-done | bytes 4194336 | tf_op jit(solution)/shard_map/all_to_all | solution.py:39
  106.9 3.4 reduce_sum.9
  110.3 4.8 %fusion.48 = (f32[512,1024]{1,0:T(8,128)}, f32[512,1024]{1,0:T(8,128)}) fusion(f32[512,3072]{1,0:T(8,128)} %all-gather.2.cloned.1.call-done), kind=kLoop, calls=%fused_computation.64 | loop fusion | bytes 8388608 | tf_op jit(solution)/shard_map/slice | solution.py:31
  115.1 3.0 reshape.44
  118.2 1.6 fusion.50
  119.8 3.1 fusion.27
  123.0 1.1 fusion.1
  124.1 1.1 fusion.2
  125.3 1.1 maximum_multiply_fusion
  126.4 0.0 all-reduce.4.cloned.1.call-update
  126.4 0.0 all-reduce.6.cloned.1.call-start
  126.5 76.0 %all-reduce.4.cloned.1.call-done = f32[2,512,256]{1,2,0:T(8,128)} async-done(((f32[2,512,256]{1,2,0:T(8,128)}), f32[2,512,256]{1,2,0:T(8,128)}) %all-reduce.4.cloned.1.call-update) | async-done | bytes 1048592 | tf_op jit(solution)/shard_map/psum | solution.py:16
  202.5 0.0 all-reduce.6.cloned.1.call-update
  202.5 0.0 all-reduce.8.cloned.1.call-start
  202.6 59.7 %all-reduce.6.cloned.1.call-done = f32[2,512,256]{1,2,0:T(8,128)} async-done(((f32[2,512,256]{1,2,0:T(8,128)}), f32[2,512,256]{1,2,0:T(8,128)}) %all-reduce.6.cloned.1.call-update) | async-done | bytes 1048592 | tf_op jit(solution)/shard_map/psum | solution.py:16
  262.3 0.0 all-reduce.8.cloned.1.call-update
  262.3 42.9 %all-reduce.8.cloned.1.call-done = f32[2,512,256]{1,2,0:T(8,128)} async-done(((f32[2,512,256]{1,2,0:T(8,128)}), f32[2,512,256]{1,2,0:T(8,128)}) %all-reduce.8.cloned.1.call-update) | async-done | bytes 1048592 | tf_op jit(solution)/shard_map/psum | solution.py:16
  305.2 2.1 collective-permute-start
  307.3 24.5 %collective-permute-done = f32[2,512,256]{1,2,0:T(8,128)S(1)} collective-permute-done((f32[2,512,256]{1,2,0:T(8,128)}, f32[2,512,256]{1,2,0:T(8,128)S(1)}, u32[]{:S(2)}, u32[]{:S(2)}) %collective-permute-start) | collective-permute-done | bytes 1048608 | tf_op jit(solution)/shard_map/ppermute | solution.py:23
  331.7 1.4 add.32
  333.2 3.0 collective-permute-start.1
  336.2 47.2 %collective-permute-done.1 = f32[2,512,256]{1,2,0:T(8,128)S(1)} collective-permute-done((f32[2,512,256]{1,2,0:T(8,128)S(1)}, f32[2,512,256]{1,2,0:T(8,128)S(1)}, u32[]{:S(2)}, u32[]{:S(2)}) %collective-permute-start.1) | collective-permute-done | bytes 1048608 | tf_op jit(solution)/shard_map/ppermute | solution.py:23
  383.4 1.2 add.33
  384.7 6.1 %collective-permute-start.2 = (f32[2,512,256]{1,2,0:T(8,128)}, f32[2,512,256]{1,2,0:T(8,128)}, u32[]{:S(2)}, u32[]{:S(2)}) collective-permute-start(f32[2,512,256]{1,2,0:T(8,128)} %add.33), channel_id=1, source_target_pairs={{0,256},{64,320},{128,384},{192,448},{256,0},{320,64},{384,128},{4... | collective-permute-start | bytes 3145736 | tf_op jit(solution)/shard_map/ppermute | solution.py:23
  390.8 4.2 reshape.45
  395.0 4.2 fusion.49
  399.2 38.5 %collective-permute-done.2 = f32[2,512,256]{1,2,0:T(8,128)} collective-permute-done((f32[2,512,256]{1,2,0:T(8,128)}, f32[2,512,256]{1,2,0:T(8,128)}, u32[]{:S(2)}, u32[]{:S(2)}) %collective-permute-start.2) | collective-permute-done | bytes 1048608 | tf_op jit(solution)/shard_map/ppermute | solution.py:23
  437.7 1.7 add.34
  439.4 1.0 fusion.13
  440.5 1.1 fusion.23
  441.6 1.0 fusion.7
  442.7 1.8 fusion.5
  444.5 1.0 convolution_subtract_fusion.2
  445.5 0.0 copy-start.9
  445.5 1.8 fusion.11
  447.4 1.0 convolution_subtract_fusion.1
  448.4 1.0 convolution_subtract_fusion
  449.4 2.1 fusion.25
  451.4 1.8 fusion.3
  453.3 0.6 dynamic-slice_bitcast_fusion.2
  453.9 1.1 convolution_bitcast_fusion
  455.0 1.0 copy.27
  456.0 0.7 pad_maximum_fusion.1
  (38 shorter events, 0.2 us)
Async XLA Ops:
  7.2 10.4 %copy-start = (f32[1,1,1,512,512]{4,3,2,1,0:T(8,128)S(1)}, f32[1,1,1,512,512]{4,3,2,1,0:T(8,128)}, u32[]{:S(2)}) copy-start(f32[1,1,1,512,512]{4,3,2,1,0:T(8,128)} %param.12) | copy-start | bytes 3145732
  7.2 103.1 %all-gather.2.cloned.1.call-start = ((), (), s32[]{:S(2)}) async-start(), calls=%async_computation.1 | async-start | bytes 7077888 | tf_op jit(solution)/shard_map/all_gather | solution.py:29
  16.8 0.8 copy-start.7
  19.7 13.5 %copy-start.14 = (f32[2,64,256]{2,1,0:T(8,128)S(1)}, f32[2,64,256]{2,1,0:T(8,128)}, u32[]{:S(2)}) copy-start(f32[2,64,256]{2,1,0:T(8,128)} %param.17) | copy-start | bytes 393220
  22.1 84.8 %all-to-all-start = ((f32[8,512,256]{2,1,0:T(8,128)}), f32[8,512,256]{2,1,0:T(8,128)}, u32[]{:S(2)}, u32[]{:S(2)}) async-start(f32[8,512,256]{2,1,0:T(8,128)} %broadcast_in_dim.9), calls=%async_computation | async-start | bytes 8388608 | tf_op jit(solution)/shard_map/all_to_all | solution.py:39
  33.1 169.4 %all-reduce.4.cloned.1.call-start = ((), (), s32[]{:S(2)}) async-start(), calls=%async_computation.2 | async-start | bytes 2097152 | tf_op jit(solution)/shard_map/psum | solution.py:16
  34.8 0.8 copy-start.12
  37.0 78.1 %copy-start.10 = (f32[512,256]{0,1:T(8,128)}, f32[512,256]{0,1:T(8,128)S(1)}, u32[]{:S(2)}) copy-start(f32[512,256]{0,1:T(8,128)S(1)} %dynamic_update_slice.10) | copy-start | bytes 1572868
  118.2 4.8 %copy-start.13 = (f32[512,256]{0,1:T(8,128)S(1)}, f32[512,256]{0,1:T(8,128)}, u32[]{:S(2)}) copy-start(f32[512,256]{0,1:T(8,128)} %copy-done.12) | copy-start | bytes 1572868
  118.2 6.0 %copy-start.11 = (f32[512,256]{0,1:T(8,128)S(1)}, f32[512,256]{0,1:T(8,128)}, u32[]{:S(2)}) copy-start(f32[512,256]{0,1:T(8,128)} %copy-done.10) | copy-start | bytes 1572868
  119.8 3.1 copy-start.1
  119.8 4.3 copy-start.3
  122.9 2.3 copy-start.5
  126.4 135.8 %all-reduce.6.cloned.1.call-start = ((), (), s32[]{:S(2)}) async-start(), calls=%async_computation.3 | async-start | bytes 2097152 | tf_op jit(solution)/shard_map/psum | solution.py:16
  202.5 102.6 %all-reduce.8.cloned.1.call-start = ((), (), s32[]{:S(2)}) async-start(), calls=%async_computation.4 | async-start | bytes 2097152 | tf_op jit(solution)/shard_map/psum | solution.py:16
  305.2 26.6 %collective-permute-start = (f32[2,512,256]{1,2,0:T(8,128)}, f32[2,512,256]{1,2,0:T(8,128)S(1)}, u32[]{:S(2)}, u32[]{:S(2)}) collective-permute-start(f32[2,512,256]{1,2,0:T(8,128)} %all-reduce.8.cloned.1.call-done), channel_id=1, source_target_pairs={{0,64},{64,0},{128,192},{192,128},{256,320},{320,256},{384,448},{4... | collective-permute-start | bytes 3145736 | tf_op jit(solution)/shard_map/ppermute | solution.py:23
  333.2 50.3 %collective-permute-start.1 = (f32[2,512,256]{1,2,0:T(8,128)S(1)}, f32[2,512,256]{1,2,0:T(8,128)S(1)}, u32[]{:S(2)}, u32[]{:S(2)}) collective-permute-start(f32[2,512,256]{1,2,0:T(8,128)S(1)} %add.32), channel_id=1, source_target_pairs={{0,128},{64,192},{128,0},{192,64},{256,384},{320,448},{384,256},{4... | collective-permute-start | bytes 3145736 | tf_op jit(solution)/shard_map/ppermute | solution.py:23
  384.7 53.0 %collective-permute-start.2 = (f32[2,512,256]{1,2,0:T(8,128)}, f32[2,512,256]{1,2,0:T(8,128)}, u32[]{:S(2)}, u32[]{:S(2)}) collective-permute-start(f32[2,512,256]{1,2,0:T(8,128)} %add.33), channel_id=1, source_target_pairs={{0,256},{64,320},{128,384},{192,448},{256,0},{320,64},{384,128},{4... | collective-permute-start | bytes 3145736 | tf_op jit(solution)/shard_map/ppermute | solution.py:23
  390.8 49.7 %slice-start = ((s8[6291456]{0:T(1024)(128)(4,1)}), s8[2097152]{0:T(1024)(128)(4,1)S(1)}, s32[]{:S(2)}) async-start(s8[6291456]{0:T(1024)(128)(4,1)} %bitcast.90), calls=%async_computation.5 | async-start | bytes 4194304
  395.0 45.5 %slice-start.1 = ((s8[6291456]{0:T(1024)(128)(4,1)}), s8[4194304]{0:T(1024)(128)(4,1)S(1)}, s32[]{:S(2)}) async-start(s8[6291456]{0:T(1024)(128)(4,1)} %bitcast.90), calls=%async_computation.6 | async-start | bytes 8388608
  440.5 6.9 %copy-start.4 = (f32[1,1,1,512,512]{4,0,3,2,1:T(1,128)S(1)}, f32[1,1,1,512,512]{4,0,3,2,1:T(1,128)}, u32[]{:S(2)}) copy-start(f32[1,1,1,512,512]{4,0,3,2,1:T(1,128)} %copy-done.3) | copy-start | bytes 3145732
  440.5 6.9 %copy-start.6 = (f32[512,256]{1,0:T(8,128)S(1)}, f32[512,256]{1,0:T(8,128)}, u32[]{:S(2)}) copy-start(f32[512,256]{1,0:T(8,128)} %copy-done.5) | copy-start | bytes 1572868
  441.6 6.7 %copy-start.2 = (f32[1,1,1,512,512]{4,0,3,2,1:T(1,128)S(1)}, f32[1,1,1,512,512]{4,0,3,2,1:T(1,128)}, u32[]{:S(2)}) copy-start(f32[1,1,1,512,512]{4,0,3,2,1:T(1,128)} %copy-done.1) | copy-start | bytes 3145732
  444.5 7.0 %copy-start.8 = (f32[512,256]{1,0:T(8,128)S(1)}, f32[512,256]{1,0:T(8,128)}, u32[]{:S(2)}) copy-start(f32[512,256]{1,0:T(8,128)} %copy-done.7) | copy-start | bytes 1572868
  445.5 8.4 %copy-start.9 = (f32[1,1,1,512,512]{4,3,2,1,0:T(8,128)S(1)}, f32[1,1,1,512,512]{4,3,2,1,0:T(8,128)}, u32[]{:S(2)}) copy-start(f32[1,1,1,512,512]{4,3,2,1,0:T(8,128)} %param.11) | copy-start | bytes 3145732
Sparse Core Ops, SparseCore 0:
  11.6 85.2 all-gather.1
  126.6 75.9 all-reduce.3
  204.9 57.3 all-reduce.5
  265.0 40.1 all-reduce.7
where the time goes:
time: 464 us; the launch traced here: 463 us
  waiting for transfers between devices  359 us (77%)
  local copies, waits for them, and re-layouts  31.3 us (7%)
  matrix products  24.3 us (5%)
  starting transfers between devices  22.4 us (5%)
  between operations  15 us (3%)
  other arithmetic  11.5 us (2%)
    psum x3, waiting for transfers between devices, by_axis(): x = lax.psum(x, axis)  179 us
    ppermute x3, waiting for transfers between devices, from_partner(): return lax.ppermute(value, axis, pairs)  110 us
    all_to_all x1, waiting for transfers between devices, from_everyone(): return lax.all_to_all(copies, axis, split_axis=0, concat_axis=0, tiled=True)  69.9 us
    dot_general x8, matrix products, product(): jnp.dot(factor, vector, precision=PRECISE, preferred_element_type=jnp.flo...  12.3 us
    dot_general x8, matrix products, transposed_product(): lax.dot_general(factor, vector, (((0,), (0,)), ((), ())), precision=PRECI...  12 us
    ppermute x3, starting transfers between devices, from_partner(): return lax.ppermute(value, axis, pairs)  11.3 us
    all_to_all x1, starting transfers between devices, from_everyone(): return lax.all_to_all(copies, axis, split_axis=0, concat_axis=0, tiled=True)  11 us
  transfers between devices with their start and end apart: 8, of which 7 were waited for; matrix products, arithmetic and copies ran while one was open for 5% of the time, Pallas kernels for 0%

commit v1 on v0

v1 whole, which is shorter than its diff:
```python
import jax
import jax.numpy as jnp
from jax import lax
from jax.sharding import Mesh
from jax.sharding import PartitionSpec as P

GX, GC = "gcol_0", "gcol_1"
GCOL = (GX, GC)
LG = ("leaf", "grow")
PRECISE = lax.Precision.HIGHEST


def dot(a, b, ca, cb):
    return lax.dot_general(
        a, b, (((ca,), (cb,)), ((), ())), precision=PRECISE, preferred_element_type=jnp.float32
    )


def swap(x, axis):
    return lax.all_to_all(x, axis, split_axis=0, concat_axis=0, tiled=True)


def shift(x, axis, step):
    n = lax.axis_size(axis)
    return lax.ppermute(x, axis, [(s, (s + step) % n) for s in range(n)])


def spread(x, n):
    return jnp.broadcast_to(x[None], (n, *x.shape))


def split_rows(blocks, parts, rows):
    stacked = jnp.concatenate(blocks, axis=0).reshape(-1, parts, rows, blocks[0].shape[-1])
    return [stacked[:, i].reshape(-1, blocks[0].shape[-1]) for i in range(parts)]


def local(
    right_leaf,
    inverse_leaf,
    lower_leaf,
    present,
    right_middle,
    inverse_middle,
    upper_middle,
    right_top,
    inverse_top,
    upper_top,
):
    n_x, n_lg = lax.axis_size(GX), lax.axis_size(LG)
    n_g = n_x * lax.axis_size(GC)
    block, nrhs = right_leaf.shape[-2:]
    share = block // n_g
    cols = nrhs // n_g
    me = lax.axis_index(GCOL)
    il, ll, rl = inverse_leaf[0, 0, 0], lower_leaf[0, 0, 0], right_leaf[0, 0, 0]
    kept = present[0, 0, 0].astype(jnp.float32)

    with jax.named_scope("gather_w"):
        w = jnp.concatenate([inverse_middle[0, 0], upper_middle[0, 0, 0], upper_middle[1, 0, 0]], axis=0)
        w_mine = swap(spread(w, n_x), GX).reshape(-1, block)
    with jax.named_scope("gather_t"):
        t = jnp.concatenate([inverse_top[0], inverse_top[1], upper_top[0]], axis=0)
    with jax.named_scope("leaf_fwd"):
        leaf_fwd = dot(il, rl, 1, 0)
        part = dot(leaf_fwd, ll, 0, 1) * kept
        lane = lax.broadcasted_iota(jnp.int32, (1, block), 1)
        own = (lane >= me * share) & (lane < (me + 1) * share)
        rm = right_middle[0, 0].T
        part = jnp.where(own, jnp.concatenate([rm] * n_g, axis=1), 0.0) - part
        sent = jnp.concatenate([part, right_top[0].T, right_top[1].T], axis=1)
        sent = sent.reshape(n_g, cols, -1)
    with jax.named_scope("core_w"):
        w_other = shift(w_mine, GC, 1)
    with jax.named_scope("leaf_swap"):
        got = swap(sent, GCOL)
    with jax.named_scope("mid_fwd"):
        rhs = jnp.sum(got[:, :, :block], axis=0)
        rt = [
            jnp.concatenate([got[c, :, block + k * share : block + (k + 1) * share] for c in range(n_g)], axis=1)
            for k in range(2)
        ]
        im, um0, um1 = split_rows([w_mine, w_other], 3, share)
        mf = dot(rhs, im, 1, 1)
        tp = jnp.concatenate([dot(mf, um0, 1, 0), dot(mf, um1, 1, 0)], axis=1)
        pieces = tp.reshape(cols, -1, 128).swapaxes(0, 1).reshape(n_lg, -1, 128)
    with jax.named_scope("gather_t"):
        ts = [t, shift(t, GX, 1), shift(t, GX, -1), shift(t, GX, 2)]
        t_mine = jnp.concatenate(ts, axis=0)
    with jax.named_scope("top_scatter"):
        pieces = swap(pieces, LG)
        total = spread(jnp.sum(pieces, axis=0), n_lg)
    with jax.named_scope("core_t"):
        t_other = shift(t_mine, GC, 1)
        it0, it1, ut = split_rows([t_mine, t_other], 3, share)
    with jax.named_scope("top_gather"):
        total = swap(total, LG)
        total = total.reshape(-1, cols, 128).swapaxes(0, 1).reshape(cols, -1)
    with jax.named_scope("top_solve"):
        f0 = dot(rt[0] - total[:, :block], it0, 1, 1)
        f1 = dot(rt[1] - total[:, block:] - dot(f0, ut, 1, 0), it1, 1, 1)
        s1 = dot(f1, it1, 1, 0)
        s0 = dot(f0 - dot(s1, ut, 1, 1), it0, 1, 0)
    with jax.named_scope("mid_bwd"):
        mr = mf - dot(s0, um0, 1, 1) - dot(s1, um1, 1, 1)
        sm = dot(mr, im, 1, 0)
        s0 = s0.reshape(cols, n_g, share).swapaxes(0, 1)
        s1 = s1.reshape(cols, n_g, share).swapaxes(0, 1)
        back = jnp.concatenate([spread(sm, n_g), s0, s1], axis=2)
    with jax.named_scope("back_swap"):
        back = swap(back, GCOL)
    with jax.named_scope("leaf_bwd"):
        back = back.reshape(nrhs, -1)
        sm = back[:, :block]
        leaf_res = leaf_fwd - dot(ll, sm, 0, 1) * kept
        leaf_back = dot(il, leaf_res, 0, 0)
        solve_middle = lax.dynamic_slice_in_dim(sm, me * share, share, 1).T
        solve_top = jnp.stack([back[:, block + k * share : block + (k + 1) * share].T for k in range(2)])
    return (leaf_back[None, None, None], solve_middle[None, None], solve_top)


def solution(mesh):
    split = Mesh(
        mesh.devices.reshape(mesh.shape["leaf"], mesh.shape["grow"], mesh.shape["gcol"] // 2, 2),
        ("leaf", "grow", GX, GC),
    )
    in_specs = (
        P("leaf", "grow", GCOL, None, None),
        P("leaf", "grow", GCOL, None, None),
        P("leaf", "grow", GCOL, None, None),
        P("leaf", "grow", GCOL),
        P("leaf", "grow", GCOL, None),
        P("leaf", "grow", GCOL, None),
        P(None, "leaf", "grow", GCOL, None),
        P(None, GCOL, None),
        P(None, GCOL, None),
        P(None, GCOL, None),
    )
    out_specs = (
        P("leaf", "grow", GCOL, None, None),
        P("leaf", "grow", GCOL, None),
        P(None, GCOL, None),
    )
    return jax.shard_map(local, mesh=split, in_specs=in_specs, out_specs=out_specs, check_vma=False)
```

time: 464 us -> 159 us (0.34)
  waiting for transfers between devices: 359 us -> 38.4 us
  starting transfers between devices: 22.4 us -> 57.7 us
  between operations: 15 us -> 1.78 us
    psum x3 -> x0, waiting for transfers between devices: 179 us -> none  [by_axis(): x = lax.psum(x, axis)]
    ppermute x3 -> x5, waiting for transfers between devices: 110 us -> 0.01 us  [shift(): return lax.ppermute(x, axis, [(s, (s + step) % n) for s in range(n)])]
    all_to_all x1 -> x5, waiting for transfers between devices: 69.9 us -> 38.3 us  [swap(): return lax.all_to_all(x, axis, split_axis=0, concat_axis=0, tiled=True)]
    all_to_all x1 -> x5, starting transfers between devices: 11 us -> 37.6 us  [swap(): return lax.all_to_all(x, axis, split_axis=0, concat_axis=0, tiled=True)]
    ppermute x3 -> x5, starting transfers between devices: 11.3 us -> 20.1 us  [shift(): return lax.ppermute(x, axis, [(s, (s + step) % n) for s in range(n)])]
    concatenate x0 -> x6, local copies, waits for them, and re-layouts: none -> 7.45 us  [the longest x1 2.68 us: split_rows(): jnp.concatenate(blocks, axis=0)]
    reshape x3, local copies, waits for them, and re-layouts: 8.16 us -> 0.84 us  [the longest x1 0.74 us: local(): s0 = s0.reshape(cols, n_g, share).swapaxes(0, 1)]
    slice x4 -> x3, local copies, waits for them, and re-layouts: 10.6 us -> 4.01 us  [the longest x2 3.95 us: split_rows(): stacked[:, i].reshape(-1, blocks[0].shape[-1])]
  transfers between devices with their start and end apart: 8 -> 10, of which waited for: 7 -> 4; matrix products, arithmetic and copies ran while one was open for 5% -> 22% of each run, Pallas kernels for 0% -> 0%
where the time goes in v1:
time: 159 us; the launch traced here: 157 us
  starting transfers between devices  57.7 us (36%)
  waiting for transfers between devices  38.4 us (24%)
  local copies, waits for them, and re-layouts  29.7 us (19%)
  matrix products  22.6 us (14%)
  other arithmetic  7.37 us (5%)
  between operations  1.78 us (1%)
    all_to_all x5, waiting for transfers between devices, swap(): return lax.all_to_all(x, axis, split_axis=0, concat_axis=0, tiled=True)  38.3 us
    all_to_all x5, starting transfers between devices, swap(): return lax.all_to_all(x, axis, split_axis=0, concat_axis=0, tiled=True)  37.6 us
    dot_general x16, matrix products, dot(): lax.dot_general(a, b, (((ca,), (cb,)), ((), ())), precision=PRECISE, pref...  22.6 us
    ppermute x5, starting transfers between devices, shift(): return lax.ppermute(x, axis, [(s, (s + step) % n) for s in range(n)])  20.1 us
    unnamed x37, local copies, waits for them, and re-layouts  10.5 us
    slice x2, local copies, waits for them, and re-layouts, split_rows(): stacked[:, i].reshape(-1, blocks[0].shape[-1])  3.95 us
  transfers between devices with their start and end apart: 10, of which 4 were waited for; matrix products, arithmetic and copies ran while one was open for 22% of the time, Pallas kernels for 0%

profile of v1, /device:TPU:1, one launch (start us, length us, event | category | flops | bytes accessed | tf_op | source)
XLA Modules:
  0.0 157.5 jit_solution(6285242616951344803)
XLA Ops:
  0.6 1.1 slice_bitcast_fusion.3
  1.7 1.7 %pad_maximum_fusion.4 = f32[192,512]{1,0:T(8,128)} fusion(f32[64,512]{1,0:T(8,128)} %bitcast.181, f32[64,512]{1,0:T(8,128)S(1)} %get-tuple-element.46, f32[64,512]{1,0:T(8,128)S(1)} %get-tuple-element.45), kind=kLoop, calls=%fused_computation.21 | loop fusion | flops 196608 | bytes 786432 | tf_op jit(solution)/shard_map/gather_t/concatenate | solution.py:62
  3.4 4.1 %collective-permute-start.1 = (f32[192,512]{1,0:T(8,128)}, f32[192,512]{1,0:T(8,128)}, u32[]{:S(2)}, u32[]{:S(2)}) collective-permute-start(f32[192,512]{1,0:T(8,128)} %pad_maximum_fusion.4), channel_id=1, source_target_pairs={{0,2},{2,4},{4,6},{6,0},{1,3},{3,5},{5,7},{7,1},{8,10},{10,12},{12... | collective-permute-start | bytes 1179656 | tf_op jit(solution)/shard_map/gather_t/ppermute | solution.py:25
  7.5 3.2 %collective-permute-start.2 = (f32[192,512]{1,0:T(8,128)}, f32[192,512]{1,0:T(8,128)}, u32[]{:S(2)}, u32[]{:S(2)}) collective-permute-start(f32[192,512]{1,0:T(8,128)} %pad_maximum_fusion.4), channel_id=1, source_target_pairs={{0,6},{2,0},{4,2},{6,4},{1,7},{3,1},{5,3},{7,5},{8,14},{10,8},{12,... | collective-permute-start | bytes 1179656 | tf_op jit(solution)/shard_map/gather_t/ppermute | solution.py:25
  10.7 3.6 %collective-permute-start.3 = (f32[192,512]{1,0:T(8,128)}, f32[192,512]{1,0:T(8,128)}, u32[]{:S(2)}, u32[]{:S(2)}) collective-permute-start(f32[192,512]{1,0:T(8,128)} %pad_maximum_fusion.4), channel_id=1, source_target_pairs={{0,4},{2,6},{4,0},{6,2},{1,5},{3,7},{5,1},{7,3},{8,12},{10,14},{12... | collective-permute-start | bytes 1179656 | tf_op jit(solution)/shard_map/gather_t/ppermute | solution.py:25
  14.3 1.0 slice_bitcast_fusion.5
  15.3 0.9 pad_maximum_fusion.3
  16.2 1.4 broadcast_in_dim.38
  17.6 3.6 %all-to-all-start.1 = ((f32[4,192,512]{2,1,0:T(8,128)}), f32[4,192,512]{2,1,0:T(8,128)S(1)}, u32[]{:S(2)}, u32[]{:S(2)}) async-start(f32[4,192,512]{2,1,0:T(8,128)} %broadcast_in_dim.38), calls=%async_computation.1 | async-start | bytes 3145728 | tf_op jit(solution)/shard_map/gather_w/all_to_all | solution.py:20
  22.0 2.3 %fusion.6 = f32[512,256]{1,0:T(8,128)S(1)} fusion(f32[1,1,1,512,512]{4,3,2,1,0:T(8,128)} %param.11, f32[1,1,1,512,256]{4,3,2,1,0:T(8,128)} %param.10), kind=kOutput, calls=%fused_computation.14 | convolution fusion | flops 805306368 | bytes 2097152 | tf_op jit(solution)/shard_map/leaf_fwd/dot_general | solution.py:14
  24.3 0.8 copy-done.5
  25.1 1.8 %fusion.1 = f32[256,512]{0,1:T(8,128)} fusion(f32[512,256]{1,0:T(8,128)S(1)} %fusion.6, f32[1,1,1,512,512]{4,3,2,1,0:T(8,128)S(1)} %copy-done, f32[256,512]{0,1:T(8,128)S(1)} %bitcast_dynamic-update-slice_fusion.7, f32[]{:T(128)} %bitcast.5, pred[512]{0:T(512)(128)(4,1)S(1)} %fusion.10), kind=kOutput, calls=%fused_computation.4 | convolution fusion | flops 805699584 | bytes 2621956 | tf_op jit(solution)/shard_map/leaf_fwd/dot_general | solution.py:14
  27.0 14.4 %all-to-all-done.1 = f32[4,192,512]{2,1,0:T(8,128)S(1)} async-done(((f32[4,192,512]{2,1,0:T(8,128)}), f32[4,192,512]{2,1,0:T(8,128)S(1)}, u32[]{:S(2)}, u32[]{:S(2)}) %all-to-all-start.1) | async-done | bytes 1572896 | tf_op jit(solution)/shard_map/gather_w/all_to_all | solution.py:20
  41.4 7.3 %collective-permute-start = (f32[768,512]{1,0:T(8,128)S(1)}, f32[768,512]{1,0:T(8,128)}, u32[]{:S(2)}, u32[]{:S(2)}) collective-permute-start(f32[768,512]{1,0:T(8,128)S(1)} %bitcast.173), channel_id=1, source_target_pairs={{0,1},{1,0},{2,3},{3,2},{4,5},{5,4},{6,7},{7,6},{8,9},{9,8},{10,11... | collective-permute-start | bytes 4718600 | tf_op jit(solution)/shard_map/core_w/ppermute | solution.py:25
  48.7 0.9 slice_bitcast_fusion.7
  49.5 1.1 pad_maximum_fusion.1
  50.6 1.1 copy.34
  51.7 4.6 %all-to-all-start = ((f32[8,32,640]{2,1,0:T(8,128)}), f32[8,32,640]{2,1,0:T(8,128)S(1)}, u32[]{:S(2)}, u32[]{:S(2)}) async-start(f32[8,32,640]{2,1,0:T(8,128)} %bitcast.178), calls=%async_computation | async-start | bytes 1310720 | tf_op jit(solution)/shard_map/leaf_swap/all_to_all | solution.py:20
  56.3 0.7 constant_dynamic-update-slice_fusion.5
  57.1 0.7 constant_dynamic-update-slice_fusion.4
  57.8 1.6 %constant_dynamic-update-slice_fusion.3 = (f32[768,512]{1,0:T(8,128)}, f32[1536,512]{1,0:T(8,128)}) fusion(f32[768,512]{1,0:T(8,128)} %get-tuple-element.41, f32[1,64,512]{2,1,0:T(8,128)} %param.19, f32[1536,512]{1,0:T(8,128)} %get-tuple-element.42), kind=kLoop, calls=%fused_computation.51 | loop fusion | bytes 393216
  59.4 2.0 %constant_dynamic-update-slice_fusion.2 = (f32[768,512]{1,0:T(8,128)}, f32[1536,512]{1,0:T(8,128)}) fusion(f32[768,512]{1,0:T(8,128)} %get-tuple-element.49, f32[192,512]{1,0:T(8,128)} %collective-permute-done.1, f32[1536,512]{1,0:T(8,128)} %get-tuple-element.50), kind=kLoop, calls=%fused_computation.50 | loop fusion | bytes 1179648
  61.4 2.0 %constant_dynamic-update-slice_fusion.1 = (f32[768,512]{1,0:T(8,128)}, f32[1536,512]{1,0:T(8,128)}) fusion(f32[768,512]{1,0:T(8,128)} %get-tuple-element.37, f32[192,512]{1,0:T(8,128)} %collective-permute-done.2, f32[1536,512]{1,0:T(8,128)} %get-tuple-element.38), kind=kLoop, calls=%fused_computation.49 | loop fusion | bytes 1179648
  63.5 2.0 %constant_dynamic-update-slice_fusion = (f32[768,512]{1,0:T(8,128)}, f32[1536,512]{1,0:T(8,128)}) fusion(f32[768,512]{1,0:T(8,128)} %get-tuple-element.35, f32[192,512]{1,0:T(8,128)} %collective-permute-done.3, f32[1536,512]{1,0:T(8,128)} %get-tuple-element.36), kind=kLoop, calls=%fused_computation.48 | loop fusion | bytes 1179648 | tf_op jit(solution)/shard_map/gather_t/concatenate | solution.py:88
  65.5 1.9 %collective-permute-start.4 = (f32[768,512]{1,0:T(8,128)}, f32[768,512]{1,0:T(8,128)}, u32[]{:S(2)}, u32[]{:S(2)}) collective-permute-start(f32[768,512]{1,0:T(8,128)} %get-tuple-element.33), channel_id=1, source_target_pairs={{0,1},{1,0},{2,3},{3,2},{4,5},{5,4},{6,7},{7,6},{8,9},{9,8},{10,11... | collective-permute-start | bytes 4718600 | tf_op jit(solution)/shard_map/core_t/ppermute | solution.py:25
  67.4 1.9 %pad_maximum_fusion = f32[1536,512]{1,0:T(8,128)S(1)} fusion(f32[768,512]{1,0:T(8,128)} %collective-permute-done, f32[768,512]{1,0:T(8,128)S(1)} %bitcast.174), kind=kLoop, calls=%fused_computation | loop fusion | flops 786432 | bytes 6291456 | tf_op jit(solution)/shard_map/mid_fwd/concatenate | solution.py:33
  69.4 0.3 fusion.13
  69.7 1.0 fusion.14
  70.8 0.7 fusion.16
  71.5 0.7 fusion.15
  72.2 0.7 copy_bitcast_fusion.1
  72.9 15.7 %all-to-all-start.2 = ((f32[64,4,128]{2,1,0:T(4,128)}), f32[64,4,128]{2,1,0:T(4,128)S(1)}, u32[]{:S(2)}, u32[]{:S(2)}) async-start(f32[64,4,128]{2,1,0:T(4,128)} %bitcast.28), calls=%async_computation.2 | async-start | bytes 262144 | tf_op jit(solution)/shard_map/top_scatter/all_to_all | solution.py:20
  88.5 1.6 %slice_bitcast_fusion.8 = (f32[32,64]{1,0:T(8,128)S(1)}, f32[32,64]{1,0:T(8,128)S(1)}, f32[32,64]{1,0:T(8,128)S(1)}, f32[32,64]{1,0:T(8,128)S(1)}, f32[32,64]{1,...) fusion(f32[8,32,640]{2,1,0:T(8,128)} %copy-done.8), kind=kLoop, calls=%fused_computation.61 | loop fusion | bytes 262144 | tf_op jit(solution)/shard_map/mid_fwd/squeeze | solution.py:79
  90.1 0.9 concatenate.39
  91.0 0.8 concatenate.44
  91.9 2.7 %constant_dynamic-update-slice_fusion.6 = f32[1536,512]{1,0:T(8,128)} fusion(f32[1536,512]{1,0:T(8,128)} %get-tuple-element.34, f32[768,512]{1,0:T(8,128)} %collective-permute-done.4), kind=kLoop, calls=%fused_computation.54 | loop fusion | bytes 3145728 | tf_op jit(solution)/shard_map/core_t/concatenate | solution.py:33
  94.5 5.5 %all-to-all-done.2 = f32[64,4,128]{2,1,0:T(4,128)S(1)} async-done(((f32[64,4,128]{2,1,0:T(4,128)}), f32[64,4,128]{2,1,0:T(4,128)S(1)}, u32[]{:S(2)}, u32[]{:S(2)}) %all-to-all-start.2) | async-done | bytes 131104 | tf_op jit(solution)/shard_map/top_scatter/all_to_all | solution.py:20
  100.0 0.1 reduce_sum.19
  100.1 0.7 broadcast_in_dim.39
  100.8 6.8 %all-to-all-start.3 = ((f32[64,4,128]{2,1,0:T(4,128)}), f32[64,4,128]{2,1,0:T(4,128)S(1)}, u32[]{:S(2)}, u32[]{:S(2)}) async-start(f32[64,4,128]{2,1,0:T(4,128)} %broadcast_in_dim.39), calls=%async_computation.3 | async-start | bytes 262144 | tf_op jit(solution)/shard_map/top_gather/all_to_all | solution.py:20
  107.6 3.6 %fusion.12 = (f32[8,1,64,512]{3,2,1,0:T(8,128)}, f32[8,1,64,512]{3,2,1,0:T(8,128)S(1)}, f32[8,1,64,512]{3,2,1,0:T(8,128)}) fusion(f32[8,3,64,512]{3,2,1,0:T(8,128)} %bitcast.34), kind=kLoop, calls=%fused_computation.81 | loop fusion | bytes 6291456 | tf_op jit(solution)/shard_map/core_t/slice | solution.py:34
  111.3 7.7 %all-to-all-done.3 = f32[64,4,128]{2,1,0:T(4,128)S(1)} async-done(((f32[64,4,128]{2,1,0:T(4,128)}), f32[64,4,128]{2,1,0:T(4,128)S(1)}, u32[]{:S(2)}, u32[]{:S(2)}) %all-to-all-start.3) | async-done | bytes 131104 | tf_op jit(solution)/shard_map/top_gather/all_to_all | solution.py:20
  119.0 2.3 %fusion.9 = f32[32,512]{1,0:T(8,128)S(1)} fusion(f32[512,512]{1,0:T(8,128)} %bitcast.169, f32[32,512]{1,0:T(8,128)S(1)} %concatenate.39, f32[32,1024]{1,0:T(8,128)S(1)} %bitcast.179), kind=kOutput, calls=%fused_computation.37 | convolution fusion | flops 100679680 | bytes 1245184 | tf_op jit(solution)/shard_map/top_solve/dot_general | solution.py:14
  121.3 0.7 convolution_subtract_fusion.3
  122.0 1.0 fusion.17
  123.1 0.7 fusion.18
  123.8 0.1 reshape.63
  123.9 1.0 convolution_subtract_fusion.2
  125.0 2.0 %fusion.19 = f32[32,512]{1,0:T(8,128)S(1)} fusion(f32[32,512]{1,0:T(8,128)S(1)} %convolution_subtract_fusion.2, f32[512,512]{1,0:T(8,128)} %bitcast.170), kind=kOutput, calls=%fused_computation.88 | convolution fusion | flops 100663296 | bytes 1179648 | tf_op jit(solution)/shard_map/top_solve/dot_general | solution.py:14
  127.0 0.7 reshape.62
  127.7 2.3 %convolution_subtract_fusion.1 = f32[32,512]{1,0:T(8,128)S(1)} fusion(f32[32,512]{1,0:T(8,128)S(1)} %fusion.14, f32[32,512]{1,0:T(8,128)S(1)} %fusion.19, f32[512,512]{1,0:T(8,128)} %bitcast.168), kind=kOutput, calls=%fused_computation.8 | convolution fusion | flops 100679680 | bytes 1245184 | tf_op jit(solution)/shard_map/mid_bwd/dot_general | solution.py:14
  130.0 1.0 convolution_subtract_fusion
  131.1 0.7 fusion.20
  131.8 0.1 copy_bitcast_fusion.2
  131.9 1.0 pad_maximum_fusion.2
  132.9 7.0 %all-to-all-start.4 = ((f32[8,32,640]{2,1,0:T(8,128)}), f32[8,32,640]{2,1,0:T(8,128)S(1)}, u32[]{:S(2)}, u32[]{:S(2)}) async-start(f32[8,32,640]{2,1,0:T(8,128)} %pad_maximum_fusion.2), calls=%async_computation.4 | async-start | bytes 1310720 | tf_op jit(solution)/shard_map/back_swap/all_to_all | solution.py:20
  139.8 10.8 %all-to-all-done.4 = f32[8,32,640]{2,1,0:T(8,128)S(1)} async-done(((f32[8,32,640]{2,1,0:T(8,128)}), f32[8,32,640]{2,1,0:T(8,128)S(1)}, u32[]{:S(2)}, u32[]{:S(2)}) %all-to-all-start.4) | async-done | bytes 655392 | tf_op jit(solution)/shard_map/back_swap/all_to_all | solution.py:20
  150.6 1.8 %fusion.2 = f32[512,256]{1,0:T(8,128)S(1)} fusion(f32[512,256]{1,0:T(8,128)S(1)} %copy-done.6, f32[1,1,1,512,512]{4,3,2,1,0:T(8,128)S(1)} %copy-done, f32[]{:T(128)} %bitcast.5, f32[256,640]{1,0:T(8,128)S(1)} %bitcast.175), kind=kOutput, calls=%fused_computation.5 | convolution fusion | flops 805568512 | bytes 2621444 | tf_op jit(solution)/shard_map/leaf_bwd/dot_general | solution.py:14
  152.5 0.1 slice_bitcast_fusion.1
  152.6 2.3 %convolution_bitcast_fusion = f32[1,1,1,512,256]{3,4,2,1,0:T(8,128)S(1)} fusion(f32[512,256]{1,0:T(8,128)S(1)} %fusion.2, f32[1,1,1,512,512]{4,3,2,1,0:T(8,128)} %param.11), kind=kOutput, calls=%fused_computation.6 | convolution fusion | flops 805306368 | bytes 2097152 | tf_op jit(solution)/shard_map/leaf_bwd/dot_general | solution.py:14
  154.9 1.0 copy.39
  155.9 0.1 dynamic-slice_bitcast_fusion
  156.0 0.7 copy.40
  156.7 0.8 copy.41
  (41 shorter events, 0.3 us)
Async XLA Ops:
  0.6 24.5 %copy-start = (f32[1,1,1,512,512]{4,3,2,1,0:T(8,128)S(1)}, f32[1,1,1,512,512]{4,3,2,1,0:T(8,128)}, u32[]{:S(2)}) copy-start(f32[1,1,1,512,512]{4,3,2,1,0:T(8,128)} %param.12) | copy-start | bytes 3145732
  3.4 17.8 %copy-start.7 = (f32[1,1,64,256]{3,2,1,0:T(8,128)S(1)}, f32[1,1,64,256]{3,2,1,0:T(8,128)}, u32[]{:S(2)}) copy-start(f32[1,1,64,256]{3,2,1,0:T(8,128)} %param.14) | copy-start | bytes 196612
  3.4 56.0 %collective-permute-start.1 = (f32[192,512]{1,0:T(8,128)}, f32[192,512]{1,0:T(8,128)}, u32[]{:S(2)}, u32[]{:S(2)}) collective-permute-start(f32[192,512]{1,0:T(8,128)} %pad_maximum_fusion.4), channel_id=1, source_target_pairs={{0,2},{2,4},{4,6},{6,0},{1,3},{3,5},{5,7},{7,1},{8,10},{10,12},{12... | collective-permute-start | bytes 1179656 | tf_op jit(solution)/shard_map/gather_t/ppermute | solution.py:25
  7.5 54.0 %collective-permute-start.2 = (f32[192,512]{1,0:T(8,128)}, f32[192,512]{1,0:T(8,128)}, u32[]{:S(2)}, u32[]{:S(2)}) collective-permute-start(f32[192,512]{1,0:T(8,128)} %pad_maximum_fusion.4), channel_id=1, source_target_pairs={{0,6},{2,0},{4,2},{6,4},{1,7},{3,1},{5,3},{7,5},{8,14},{10,8},{12,... | collective-permute-start | bytes 1179656 | tf_op jit(solution)/shard_map/gather_t/ppermute | solution.py:25
  10.7 52.8 %collective-permute-start.3 = (f32[192,512]{1,0:T(8,128)}, f32[192,512]{1,0:T(8,128)}, u32[]{:S(2)}, u32[]{:S(2)}) collective-permute-start(f32[192,512]{1,0:T(8,128)} %pad_maximum_fusion.4), channel_id=1, source_target_pairs={{0,4},{2,6},{4,0},{6,2},{1,5},{3,7},{5,1},{7,3},{8,12},{10,14},{12... | collective-permute-start | bytes 1179656 | tf_op jit(solution)/shard_map/gather_t/ppermute | solution.py:25
  17.6 23.8 %all-to-all-start.1 = ((f32[4,192,512]{2,1,0:T(8,128)}), f32[4,192,512]{2,1,0:T(8,128)S(1)}, u32[]{:S(2)}, u32[]{:S(2)}) async-start(f32[4,192,512]{2,1,0:T(8,128)} %broadcast_in_dim.38), calls=%async_computation.1 | async-start | bytes 3145728 | tf_op jit(solution)/shard_map/gather_w/all_to_all | solution.py:20
  24.3 0.8 copy-start.5
  25.1 31.2 %copy-start.9 = (f32[2,64,512]{2,1,0:T(8,128)S(1)}, f32[2,64,512]{2,1,0:T(8,128)}, u32[]{:S(2)}) copy-start(f32[2,64,512]{2,1,0:T(8,128)} %param.18) | copy-start | bytes 786436
  41.4 26.1 %collective-permute-start = (f32[768,512]{1,0:T(8,128)S(1)}, f32[768,512]{1,0:T(8,128)}, u32[]{:S(2)}, u32[]{:S(2)}) collective-permute-start(f32[768,512]{1,0:T(8,128)S(1)} %bitcast.173), channel_id=1, source_target_pairs={{0,1},{1,0},{2,3},{3,2},{4,5},{5,4},{6,7},{7,6},{8,9},{9,8},{10,11... | collective-permute-start | bytes 4718600 | tf_op jit(solution)/shard_map/core_w/ppermute | solution.py:25
  51.7 15.7 %all-to-all-start = ((f32[8,32,640]{2,1,0:T(8,128)}), f32[8,32,640]{2,1,0:T(8,128)S(1)}, u32[]{:S(2)}, u32[]{:S(2)}) async-start(f32[8,32,640]{2,1,0:T(8,128)} %bitcast.178), calls=%async_computation | async-start | bytes 1310720 | tf_op jit(solution)/shard_map/leaf_swap/all_to_all | solution.py:20
  65.5 26.4 %collective-permute-start.4 = (f32[768,512]{1,0:T(8,128)}, f32[768,512]{1,0:T(8,128)}, u32[]{:S(2)}, u32[]{:S(2)}) collective-permute-start(f32[768,512]{1,0:T(8,128)} %get-tuple-element.33), channel_id=1, source_target_pairs={{0,1},{1,0},{2,3},{3,2},{4,5},{5,4},{6,7},{7,6},{8,9},{9,8},{10,11... | collective-permute-start | bytes 4718600 | tf_op jit(solution)/shard_map/core_t/ppermute | solution.py:25
  67.4 2.0 %copy-start.8 = (f32[8,32,640]{2,1,0:T(8,128)}, f32[8,32,640]{2,1,0:T(8,128)S(1)}, u32[]{:S(2)}) copy-start(f32[8,32,640]{2,1,0:T(8,128)S(1)} %all-to-all-done) | copy-start | bytes 1966084
  69.7 1.8 %copy-start.3 = (f32[8,1,64,512]{3,2,1,0:T(8,128)}, f32[8,1,64,512]{3,2,1,0:T(8,128)S(1)}, u32[]{:S(2)}) copy-start(f32[8,1,64,512]{3,2,1,0:T(8,128)S(1)} %get-tuple-element.12) | copy-start | bytes 3145732
  69.7 24.9 %copy-start.1 = (f32[8,1,64,512]{3,2,1,0:T(8,128)}, f32[8,1,64,512]{3,2,1,0:T(8,128)S(1)}, u32[]{:S(2)}) copy-start(f32[8,1,64,512]{3,2,1,0:T(8,128)S(1)} %get-tuple-element.13) | copy-start | bytes 3145732
  72.9 27.2 %all-to-all-start.2 = ((f32[64,4,128]{2,1,0:T(4,128)}), f32[64,4,128]{2,1,0:T(4,128)S(1)}, u32[]{:S(2)}, u32[]{:S(2)}) async-start(f32[64,4,128]{2,1,0:T(4,128)} %bitcast.28), calls=%async_computation.2 | async-start | bytes 262144 | tf_op jit(solution)/shard_map/top_scatter/all_to_all | solution.py:20
  100.8 18.2 %all-to-all-start.3 = ((f32[64,4,128]{2,1,0:T(4,128)}), f32[64,4,128]{2,1,0:T(4,128)S(1)}, u32[]{:S(2)}, u32[]{:S(2)}) async-start(f32[64,4,128]{2,1,0:T(4,128)} %broadcast_in_dim.39), calls=%async_computation.3 | async-start | bytes 262144 | tf_op jit(solution)/shard_map/top_gather/all_to_all | solution.py:20
  118.9 3.1 %copy-start.4 = (f32[8,1,64,512]{3,2,1,0:T(8,128)S(1)}, f32[8,1,64,512]{3,2,1,0:T(8,128)}, u32[]{:S(2)}) copy-start(f32[8,1,64,512]{3,2,1,0:T(8,128)} %get-tuple-element.9) | copy-start | bytes 3145732
  124.9 5.1 %copy-start.2 = (f32[8,1,64,512]{3,2,1,0:T(8,128)S(1)}, f32[8,1,64,512]{3,2,1,0:T(8,128)}, u32[]{:S(2)}) copy-start(f32[8,1,64,512]{3,2,1,0:T(8,128)} %copy-done.1) | copy-start | bytes 3145732
  127.7 4.1 %copy-start.10 = (f32[32,8,64]{2,1,0:T(8,128)S(1)}, f32[32,8,64]{2,1,0:T(8,128)}, u32[]{:S(2)}) copy-start(f32[32,8,64]{2,1,0:T(8,128)} %reshape.62) | copy-start | bytes 196612
  131.1 19.5 %copy-start.6 = (f32[512,256]{1,0:T(8,128)S(1)}, f32[512,256]{1,0:T(8,128)}, u32[]{:S(2)}) copy-start(f32[512,256]{1,0:T(8,128)} %copy-done.5) | copy-start | bytes 1572868
  132.9 17.7 %all-to-all-start.4 = ((f32[8,32,640]{2,1,0:T(8,128)}), f32[8,32,640]{2,1,0:T(8,128)S(1)}, u32[]{:S(2)}, u32[]{:S(2)}) async-start(f32[8,32,640]{2,1,0:T(8,128)} %pad_maximum_fusion.2), calls=%async_computation.4 | async-start | bytes 1310720 | tf_op jit(solution)/shard_map/back_swap/all_to_all | solution.py:20

commit v2 on v1

v2 whole, which is shorter than its diff:
```python
import jax
import jax.numpy as jnp
from jax import lax
from jax.experimental import pallas as pl
from jax.experimental.pallas import tpu as pltpu
from jax.sharding import Mesh
from jax.sharding import PartitionSpec as P

GX, GC = "gcol_0", "gcol_1"
GCOL = (GX, GC)
LG = ("leaf", "grow")
PRECISE = lax.Precision.HIGHEST


def dot(a, b, ca, cb):
    return lax.dot_general(
        a, b, (((ca,), (cb,)), ((), ())), precision=PRECISE, preferred_element_type=jnp.float32
    )


def swap(x, axis):
    return lax.all_to_all(x, axis, split_axis=0, concat_axis=0, tiled=True)


def shift(x, axis, step):
    n = lax.axis_size(axis)
    return lax.ppermute(x, axis, [(s, (s + step) % n) for s in range(n)])


def f32(*shape):
    return jax.ShapeDtypeStruct(shape, jnp.float32)


def kernel_call(body, outs, *args, scalars=0, scratch=(), limit=24):
    specs = [pl.BlockSpec(memory_space=pltpu.SMEM)] * scalars
    specs += [pl.BlockSpec(memory_space=pltpu.VMEM)] * (len(args) - scalars)
    out_specs = jax.tree.map(lambda _: pl.BlockSpec(memory_space=pltpu.VMEM), outs)
    return pl.pallas_call(
        body, out_shape=outs, in_specs=specs, out_specs=out_specs, scratch_shapes=scratch,
        compiler_params=pltpu.CompilerParams(vmem_limit_bytes=limit << 20),
    )(*args)


def split(x):
    high = x.astype(jnp.bfloat16)
    return high, (x - high.astype(jnp.float32)).astype(jnp.bfloat16)


def dot3(a, b, ca, cb):
    def one(x, y):
        return lax.dot_general(
            x, y, (((ca,), (cb,)), ((), ())), preferred_element_type=jnp.float32
        )

    (ah, al), (bh, bl) = a, b
    return one(ah, bh) + (one(ah, bl) + one(al, bh))


def pack_kernel(im, um, it, ut, w, t, sems):
    share = im.shape[0]
    copies = [
        pltpu.make_async_copy(src, out.at[pl.ds(at * share, src.shape[0])], sems.at[i])
        for i, (src, out, at) in enumerate([(im, w, 0), (um, w, 1), (it, t, 0), (ut, t, 2)])
    ]
    for c in copies:
        c.start()
    for c in copies:
        c.wait()


def fill(high, low, blocks, part, share):
    n = 0
    for ref in blocks:
        for s in range(ref.shape[0] // (3 * share)):
            at = (3 * s + part) * share
            h, l = split(ref[at : at + share])
            high[n * share : (n + 1) * share] = h
            low[n * share : (n + 1) * share] = l
            n += 1
    return high[...], low[...]


def mid_kernel(got, mine, other, pieces, mf_out, high, low):
    blocks = [mine, other]
    n_x, cols, _ = got.shape
    block = other.shape[1]
    share = mine.shape[0] // (3 * n_x)
    rhs = got[0, :, :block]
    for c in range(1, n_x):
        rhs = rhs + got[c, :, :block]
    mf = dot3(split(rhs), fill(high.at[0], low.at[0], blocks, 0, share), 1, 1)
    mf_out[...] = mf
    mfs = split(mf)
    rows = pieces.shape[1]
    per = cols // rows
    for k in range(2):
        tp = dot3(mfs, fill(high.at[1 + k], low.at[1 + k], blocks, 1 + k, share), 1, 0)
        for j in range(block // 128):
            for i in range(per):
                at = (k * (block // 128) + j) * per + i
                pieces[at] = tp[i * rows : (i + 1) * rows, j * 128 : (j + 1) * 128]


def sum_kernel(pieces, out):
    total = jnp.sum(pieces[...], axis=0)
    out[...] = jnp.broadcast_to(total[None], out.shape)


def top_kernel(got, total, mf, t_mine, t_other, mine, other, back, r, high, low, w_high, w_low):
    n_x, cols, _ = got.shape
    n_g, block = back.shape[0], other.shape[1]
    share = block // n_g
    two = 2 * share
    rows = total.shape[1]
    per = cols // rows
    for j in range(2 * block // 128):
        for i in range(per):
            r[i * rows : (i + 1) * rows, j * 128 : (j + 1) * 128] = total[j * per + i]
    for k in range(2):
        for x in range(n_x):
            at = k * block + x * two
            r[:, at : at + two] = got[x, :, block + k * two : block + (k + 1) * two] - r[:, at : at + two]
    it0, it1, ut = (
        fill(high.at[p], low.at[p], [t_mine, t_other], p, share) for p in range(3)
    )
    f0 = dot3(split(r[:, :block]), it0, 1, 1)
    f1 = dot3(split(r[:, block:] - dot3(split(f0), ut, 1, 0)), it1, 1, 1)
    s1 = dot3(split(f1), it1, 1, 0)
    s1s = split(s1)
    s0 = dot3(split(f0 - dot3(s1s, ut, 1, 1)), it0, 1, 0)
    im, um0, um1 = (fill(w_high.at[p], w_low.at[p], [mine, other], p, share) for p in range(3))
    mr = mf[...] - dot3(split(s0), um0, 1, 1) - dot3(s1s, um1, 1, 1)
    sm = dot3(split(mr), im, 1, 0)
    for d in range(n_g):
        back[d, :, :block] = sm
        back[d, :, block : block + share] = s0[:, d * share : (d + 1) * share]
        back[d, :, block + share :] = s1[:, d * share : (d + 1) * share]


def end_kernel(me, back, link, lead, leaf_out, mid_out, top_out):
    n_g, cols, _ = back.shape
    block = link.shape[0]
    share = block // n_g
    both = back[...].reshape(n_g * cols, back.shape[2])
    sm = both[:, :block]
    leaf_out[...] = lead[...] - dot3(split(link[...]), split(sm), 1, 1)
    mine = jnp.zeros((n_g * cols, share), jnp.float32)
    for c in range(n_g):
        mine = jnp.where(me[0] == c, sm[:, c * share : (c + 1) * share], mine)
    mid_out[...] = mine.T
    for k in range(2):
        top_out[k] = both[:, block + k * share : block + (k + 1) * share].T


def local(
    right_leaf,
    inverse_leaf,
    lower_leaf,
    present,
    right_middle,
    inverse_middle,
    upper_middle,
    right_top,
    inverse_top,
    upper_top,
):
    n_x, n_c, n_lg = lax.axis_size(GX), lax.axis_size(GC), lax.axis_size(LG)
    n_g = n_x * n_c
    block, nrhs = right_leaf.shape[-2:]
    share = block // n_g
    cols = nrhs // n_g
    me, core = lax.axis_index(GCOL), lax.axis_index(GC)
    il, ll, rl = inverse_leaf[0, 0, 0], lower_leaf[0, 0, 0], right_leaf[0, 0, 0]
    kept = present[0, 0, 0].astype(jnp.float32)

    any_spec = pl.BlockSpec(memory_space=pl.ANY)
    vmem_spec = pl.BlockSpec(memory_space=pltpu.VMEM)
    w, t = pl.pallas_call(
        pack_kernel,
        out_shape=(f32(3 * share, block), f32(3 * share, block)),
        in_specs=[any_spec] * 4,
        out_specs=(vmem_spec, vmem_spec),
        scratch_shapes=[pltpu.SemaphoreType.DMA((4,))],
        name="pack",
    )(inverse_middle[0, 0], upper_middle.reshape(2 * share, block), inverse_top.reshape(2 * share, block), upper_top[0])
    ws = [w, shift(w, GX, 1), shift(w, GX, -1), shift(w, GX, 2)]
    leaf_fwd = dot(il, rl, 1, 0)
    part = dot(leaf_fwd, ll, 0, 1) * kept
    lane = lax.broadcasted_iota(jnp.int32, (1, block), 1)
    own = (lane >= me * share) & (lane < (me + 1) * share)
    rm = right_middle[0, 0].T
    part = jnp.where(own, jnp.concatenate([rm] * n_g, axis=1), 0.0) - part
    first = lax.broadcasted_iota(jnp.int32, (1, n_c * share), 1) // share == core
    rts = [jnp.where(first, jnp.concatenate([right_top[k].T] * n_c, axis=1), 0.0) for k in range(2)]
    sent = jnp.concatenate([part, *rts], axis=1).reshape(n_x, n_c, cols, -1)
    keep = lax.dynamic_index_in_dim(sent, core, 1, keepdims=False)
    give = lax.dynamic_index_in_dim(sent, 1 - core, 1, keepdims=False)
    take = shift(give, GC, 1)
    keep = keep + take
    lead = dot(il, leaf_fwd, 0, 0)
    link = dot(il, ll, 0, 1) * kept
    got = swap(keep, GX)
    mine = jnp.concatenate(ws, axis=0)
    other = shift(mine, GC, 1)
    ts = [t, shift(t, GX, 1), shift(t, GX, -1), shift(t, GX, 2)]
    halves = pltpu.VMEM((3, block, block), jnp.bfloat16)
    pieces, mf = kernel_call(
        mid_kernel,
        (f32(n_lg, 2 * cols * block // 128 // n_lg, 128), f32(cols, block)),
        got, mine, other, scratch=[halves, halves],
    )
    arrived = swap(pieces, LG)
    t_mine, arrived = lax.optimization_barrier((jnp.concatenate(ts, axis=0), arrived))
    t_other = shift(t_mine, GC, 1)
    total = kernel_call(sum_kernel, pieces, arrived)
    total = swap(total, LG)
    back = kernel_call(
        top_kernel, f32(n_g, cols, block + 2 * share), got, total, mf, t_mine, t_other, mine, other,
        scratch=[pltpu.VMEM((cols, 2 * block), jnp.float32), halves, halves, halves, halves],
    )
    back = swap(back, GCOL)
    leaf_back, solve_middle, solve_top = kernel_call(
        end_kernel,
        (f32(block, nrhs), f32(share, nrhs), f32(2, share, nrhs)),
        me.reshape(1).astype(jnp.int32), back, link, lead, scalars=1,
    )
    return (leaf_back[None, None, None], solve_middle[None, None], solve_top)


def solution(mesh):
    split = Mesh(
        mesh.devices.reshape(mesh.shape["leaf"], mesh.shape["grow"], mesh.shape["gcol"] // 2, 2),
        ("leaf", "grow", GX, GC),
    )
    in_specs = (
        P("leaf", "grow", GCOL, None, None),
        P("leaf", "grow", GCOL, None, None),
        P("leaf", "grow", GCOL, None, None),
        P("leaf", "grow", GCOL),
        P("leaf", "grow", GCOL, None),
        P("leaf", "grow", GCOL, None),
        P(None, "leaf", "grow", GCOL, None),
        P(None, GCOL, None),
        P(None, GCOL, None),
        P(None, GCOL, None),
    )
    out_specs = (
        P("leaf", "grow", GCOL, None, None),
        P("leaf", "grow", GCOL, None),
        P(None, GCOL, None),
    )
    return jax.shard_map(local, mesh=split, in_specs=in_specs, out_specs=out_specs, check_vma=False)
```

time: 159 us -> 134 us (0.84)
  waiting for transfers between devices: 38.4 us -> 17 us
  local copies, waits for them, and re-layouts: 29.7 us -> 9.44 us
  blocking collectives: 0 us -> 15.7 us
  matrix products: 22.6 us -> 9.23 us
  Pallas kernels: 0 us -> 12.4 us
  starting transfers between devices: 57.7 us -> 62 us
  other arithmetic: 7.37 us -> 5.26 us
    all_to_all x5 -> x3, waiting for transfers between devices: 38.3 us -> 14.3 us  [swap(): return lax.all_to_all(x, axis, split_axis=0, concat_axis=0, tiled=True)]
    ppermute x5 -> x9, starting transfers between devices: 20.1 us -> 37.7 us  [shift(): return lax.ppermute(x, axis, [(s, (s + step) % n) for s in range(n)])]
    all_to_all x0 -> x1, blocking collectives: none -> 15.7 us  [swap(): return lax.all_to_all(x, axis, split_axis=0, concat_axis=0, tiled=True)]
    all_to_all x5 -> x3, starting transfers between devices: 37.6 us -> 24.2 us  [swap(): return lax.all_to_all(x, axis, split_axis=0, concat_axis=0, tiled=True)]
    dot_general x16 -> x4, matrix products: 22.6 us -> 9.23 us  [dot(): lax.dot_general(a, b, (((ca,), (cb,)), ((), ())), precision=PRECISE, pref...]
    pallas_call x0 -> x5, Pallas kernels: none -> 12.4 us  [the longest x4 10.3 us: kernel_call(): pl.pallas_call(body, out_shape=outs, in_specs=specs, out_specs=out_specs,...]
    concatenate x5 -> x1, local copies, waits for them, and re-layouts: 7.45 us -> 1.02 us  [local(): mine = jnp.concatenate(ws, axis=0)]
    unnamed x37 -> x26, local copies, waits for them, and re-layouts: 10.5 us -> 5.74 us
  transfers between devices with their start and end apart: 10 -> 12, of which waited for: 4 -> 4; matrix products, arithmetic and copies ran while one was open for 22% -> 16% of each run, Pallas kernels for 0% -> 3%
where the time goes in v2:
time: 134 us; the launch traced here: 133 us
  starting transfers between devices  62 us (46%)
  waiting for transfers between devices  17 us (13%)
  blocking collectives  15.7 us (12%)
  Pallas kernels  12.4 us (9%)
  local copies, waits for them, and re-layouts  9.44 us (7%)
  matrix products  9.23 us (7%)
  other arithmetic  5.26 us (4%)
  between operations  1.64 us (1%)
    ppermute x9, starting transfers between devices, shift(): return lax.ppermute(x, axis, [(s, (s + step) % n) for s in range(n)])  37.7 us
    all_to_all x3, starting transfers between devices, swap(): return lax.all_to_all(x, axis, split_axis=0, concat_axis=0, tiled=True)  24.2 us
    all_to_all x1, blocking collectives, swap(): return lax.all_to_all(x, axis, split_axis=0, concat_axis=0, tiled=True)  15.7 us
    all_to_all x3, waiting for transfers between devices, swap(): return lax.all_to_all(x, axis, split_axis=0, concat_axis=0, tiled=True)  14.3 us
    pallas_call x4, Pallas kernels, kernel_call(): pl.pallas_call(body, out_shape=outs, in_specs=specs, out_specs=out_specs,...  10.3 us
    dot_general x4, matrix products, dot(): lax.dot_general(a, b, (((ca,), (cb,)), ((), ())), precision=PRECISE, pref...  9.23 us
    unnamed x26, local copies, waits for them, and re-layouts  5.74 us
  transfers between devices with their start and end apart: 12, of which 4 were waited for; matrix products, arithmetic and copies ran while one was open for 16% of the time, Pallas kernels for 3%

profile of v2, /device:TPU:1, one launch (start us, length us, event | category | flops | bytes accessed | tf_op | source)
XLA Modules:
  0.0 132.6 jit_solution(16208769839959285614)
XLA Ops:
  0.6 0.0 copy-start
  0.6 2.1 %pack.1 = (f32[192,512]{1,0:T(8,128)}, f32[192,512]{1,0:T(8,128)}) custom-call(f32[64,512]{1,0:T(8,128)} %bitcast.59, f32[128,512]{1,0:T(8,128)} %bitcast.57, f32[128,512]{1,0:T(8,128)} %bitcast.58, f32[64,512]{1,0:T(8,128)} %bitcast.60), custom_call_target="tpu_custom_call" | custom-call | tf_op jit(solution)/shard_map/pack/pallas_call | solution.py:178
  2.8 3.9 %collective-permute-start.4 = (f32[192,512]{1,0:T(8,128)}, f32[192,512]{1,0:T(8,128)}, u32[]{:S(2)}, u32[]{:S(2)}) collective-permute-start(f32[192,512]{1,0:T(8,128)} %get-tuple-element.13), channel_id=1, source_target_pairs={{0,2},{2,4},{4,6},{6,0},{1,3},{3,5},{5,7},{7,1},{8,10},{10,12},{12... | collective-permute-start | bytes 1179656 | tf_op jit(solution)/shard_map/ppermute | solution.py:27
  6.7 3.2 %collective-permute-start.5 = (f32[192,512]{1,0:T(8,128)}, f32[192,512]{1,0:T(8,128)}, u32[]{:S(2)}, u32[]{:S(2)}) collective-permute-start(f32[192,512]{1,0:T(8,128)} %get-tuple-element.13), channel_id=1, source_target_pairs={{0,6},{2,0},{4,2},{6,4},{1,7},{3,1},{5,3},{7,5},{8,14},{10,8},{12,... | collective-permute-start | bytes 1179656 | tf_op jit(solution)/shard_map/ppermute | solution.py:27
  9.9 3.6 %collective-permute-start.6 = (f32[192,512]{1,0:T(8,128)}, f32[192,512]{1,0:T(8,128)}, u32[]{:S(2)}, u32[]{:S(2)}) collective-permute-start(f32[192,512]{1,0:T(8,128)} %get-tuple-element.13), channel_id=1, source_target_pairs={{0,4},{2,6},{4,0},{6,2},{1,5},{3,7},{5,1},{7,3},{8,12},{10,14},{12... | collective-permute-start | bytes 1179656 | tf_op jit(solution)/shard_map/ppermute | solution.py:27
  13.6 0.9 fusion.10
  14.5 0.0 copy-done
  14.5 0.0 copy-start.9
  14.5 2.1 %fusion.5 = f32[512,256]{1,0:T(8,128)S(1)} fusion(f32[1,1,1,512,512]{4,3,2,1,0:T(8,128)S(1)} %copy-done, f32[1,1,1,512,256]{4,3,2,1,0:T(8,128)} %param.10), kind=kOutput, calls=%fused_computation.9 | convolution fusion | flops 805306368 | bytes 2097152 | tf_op jit(solution)/shard_map/dot_general | solution.py:16
  16.5 0.0 copy-start.3
  16.6 0.1 copy.21
  16.7 0.1 copy.20
  16.8 0.8 maximum_select_fusion
  18.2 0.0 copy-done.9
  18.2 0.1 copy.13
  18.3 1.0 concatenate.18
  19.3 0.0 copy-start.5
  19.3 1.1 constant_dynamic-update-slice_fusion.3
  20.5 0.0 collective-permute-done.4
  20.5 1.0 constant_dynamic-update-slice_fusion.2
  21.5 0.0 collective-permute-done.5
  21.5 1.0 constant_dynamic-update-slice_fusion.1
  22.5 0.0 copy-start.8
  22.5 0.6 collective-permute-done.6
  23.2 1.0 constant_dynamic-update-slice_fusion.mine
  24.2 10.1 %collective-permute-start.7 = (f32[768,512]{1,0:T(8,128)S(1)}, f32[768,512]{1,0:T(8,128)}, u32[]{:S(2)}, u32[]{:S(2)}) collective-permute-start(f32[768,512]{1,0:T(8,128)S(1)} %constant_dynamic-update-slice_fusion.mine), channel_id=1, source_target_pairs={{0,1},{1,0},{2,3},{3,2},{4,5},{5,4},{6,7},{7,6},{8,9},{9,8},{10,11... | collective-permute-start | bytes 4718600 | tf_op jit(solution)/shard_map/ppermute | solution.py:27
  34.3 0.0 copy-done.3
  34.3 0.0 copy-done.5
  34.3 0.0 copy-done.7
  34.4 1.9 %fusion = f32[256,512]{1,0:T(8,128)S(1)} fusion(f32[512,256]{1,0:T(8,128)S(1)} %fusion.5, f32[1,1,1,512,512]{4,3,2,1,0:T(8,128)S(1)} %copy-done.5, f32[256,512]{1,0:T(8,128)S(1)} %copy-done.7, f32[]{:T(128)} %bitcast.6, pred[512]{0:T(512)(128)(4,1)S(1)} %fusion.8), kind=kOutput, calls=%fused_computation.3 | convolution fusion | flops 805699584 | bytes 2621956 | tf_op jit(solution)/shard_map/dot_general | solution.py:16
  36.2 0.0 copy-done.8
  36.2 0.1 pad_maximum_fusion.1
  36.3 0.8 dynamic-slice_bitcast_fusion
  37.1 1.9 %collective-permute-start = (f32[4,32,768]{2,1,0:T(8,128)}, f32[4,32,768]{2,1,0:T(8,128)}, u32[]{:S(2)}, u32[]{:S(2)}) collective-permute-start(f32[4,32,768]{2,1,0:T(8,128)} %dynamic-slice_bitcast_fusion), channel_id=1, source_target_pairs={{0,1},{1,0},{2,3},{3,2},{4,5},{5,4},{6,7},{7,6},{8,9},{9,8},{10,11... | collective-permute-start | bytes 1179656 | tf_op jit(solution)/shard_map/ppermute | solution.py:27
  39.0 2.0 %collective-permute-done = f32[4,32,768]{2,1,0:T(8,128)} collective-permute-done((f32[4,32,768]{2,1,0:T(8,128)}, f32[4,32,768]{2,1,0:T(8,128)}, u32[]{:S(2)}, u32[]{:S(2)}) %collective-permute-start) | collective-permute-done | bytes 393248 | tf_op jit(solution)/shard_map/ppermute | solution.py:27
  41.0 1.8 %bitcast_add_fusion = f32[4,32,768]{2,1,0:T(8,128)} fusion(f32[4,32,768]{2,1,0:T(8,128)} %collective-permute-done, f32[4,2,32,768]{3,2,1,0:T(8,128)S(1)} %bitcast.54, s32[]{:T(128)S(6)} %select_n.32), kind=kLoop, calls=%fused_computation.13 | loop fusion | flops 98304 | bytes 1179652 | tf_op jit(solution)/shard_map/add | solution.py:199
  42.8 3.5 %all-to-all-start = ((f32[4,32,768]{2,1,0:T(8,128)}), f32[4,32,768]{2,1,0:T(8,128)S(1)}, u32[]{:S(2)}, u32[]{:S(2)}) async-start(f32[4,32,768]{2,1,0:T(8,128)} %bitcast_add_fusion), calls=%async_computation | async-start | bytes 786432 | tf_op jit(solution)/shard_map/all_to_all | solution.py:22
  46.3 3.3 %collective-permute-start.1 = (f32[192,512]{1,0:T(8,128)}, f32[192,512]{1,0:T(8,128)}, u32[]{:S(2)}, u32[]{:S(2)}) collective-permute-start(f32[192,512]{1,0:T(8,128)} %get-tuple-element.12), channel_id=1, source_target_pairs={{0,2},{2,4},{4,6},{6,0},{1,3},{3,5},{5,7},{7,1},{8,10},{10,12},{12... | collective-permute-start | bytes 1179656 | tf_op jit(solution)/shard_map/ppermute | solution.py:27
  49.6 3.2 %collective-permute-start.2 = (f32[192,512]{1,0:T(8,128)}, f32[192,512]{1,0:T(8,128)}, u32[]{:S(2)}, u32[]{:S(2)}) collective-permute-start(f32[192,512]{1,0:T(8,128)} %get-tuple-element.12), channel_id=1, source_target_pairs={{0,6},{2,0},{4,2},{6,4},{1,7},{3,1},{5,3},{7,5},{8,14},{10,8},{12,... | collective-permute-start | bytes 1179656 | tf_op jit(solution)/shard_map/ppermute | solution.py:27
  52.8 3.6 %collective-permute-start.3 = (f32[192,512]{1,0:T(8,128)}, f32[192,512]{1,0:T(8,128)}, u32[]{:S(2)}, u32[]{:S(2)}) collective-permute-start(f32[192,512]{1,0:T(8,128)} %get-tuple-element.12), channel_id=1, source_target_pairs={{0,4},{2,6},{4,0},{6,2},{1,5},{3,7},{5,1},{7,3},{8,12},{10,14},{12... | collective-permute-start | bytes 1179656 | tf_op jit(solution)/shard_map/ppermute | solution.py:27
  56.4 0.0 all-to-all-done.got
  56.4 0.0 collective-permute-done.7.other
  56.5 3.3 %shard_map.121 = (f32[64,4,128]{2,1,0:T(4,128)}, f32[32,512]{1,0:T(8,128)S(1)}) custom-call(f32[4,32,768]{2,1,0:T(8,128)S(1)} %all-to-all-done.got, f32[768,512]{1,0:T(8,128)S(1)} %constant_dynamic-update-slice_fusion.mine, f32[768,512]{1,0:T(8,128)} %collective-permute-done.7.other), custom_call_target="tpu_custom_call" | custom-call | tf_op jit(solution)/shard_map/pallas_call | solution.py:38
  59.7 15.4 %all-to-all-start.1 = ((f32[64,4,128]{2,1,0:T(4,128)}), f32[64,4,128]{2,1,0:T(4,128)S(1)}, u32[]{:S(2)}, u32[]{:S(2)}) async-start(f32[64,4,128]{2,1,0:T(4,128)} %get-tuple-element.14), calls=%async_computation.1 | async-start | bytes 262144 | tf_op jit(solution)/shard_map/all_to_all | solution.py:22
  75.2 0.0 collective-permute-done.1
  75.2 0.0 collective-permute-done.2
  75.2 0.0 collective-permute-done.3
  75.2 2.6 %pad_maximum_fusion.t_mine = f32[768,512]{1,0:T(8,128)} fusion(f32[192,512]{1,0:T(8,128)} %collective-permute-done.3, f32[192,512]{1,0:T(8,128)} %collective-permute-done.2, f32[192,512]{1,0:T(8,128)} %collective-permute-done.1, f32[192,512]{1,0:T(8,128)} %get-tuple-element.12), kind=kLoop, calls=%fused_computation | loop fusion | flops 1179648 | bytes 3145728 | tf_op jit(solution)/shard_map/concatenate | solution.py:213
  77.8 8.9 %all-to-all-done.1.pieces = f32[64,4,128]{2,1,0:T(4,128)S(1)} async-done(((f32[64,4,128]{2,1,0:T(4,128)}), f32[64,4,128]{2,1,0:T(4,128)S(1)}, u32[]{:S(2)}, u32[]{:S(2)}) %all-to-all-start.1) | async-done | bytes 131104 | tf_op jit(solution)/shard_map/all_to_all | solution.py:22
  86.7 4.9 %collective-permute-start.8 = (f32[768,512]{1,0:T(8,128)}, f32[768,512]{1,0:T(8,128)S(1)}, u32[]{:S(2)}, u32[]{:S(2)}) collective-permute-start(f32[768,512]{1,0:T(8,128)} %pad_maximum_fusion.t_mine), channel_id=1, source_target_pairs={{0,1},{1,0},{2,3},{3,2},{4,5},{5,4},{6,7},{7,6},{8,9},{9,8},{10,11... | collective-permute-start | bytes 4718600 | tf_op jit(solution)/shard_map/ppermute | solution.py:27
  91.5 0.1 shard_map.122
  91.6 15.7 %all_to_all.20.total = f32[64,4,128]{2,1,0:T(4,128)S(1)} all-to-all(f32[64,4,128]{2,1,0:T(4,128)S(1)} %shard_map.122), channel_id=1, replica_groups=mesh['leaf'=8,'grow'=8,'gcol_0'=4,'gcol_1'=2] {'leaf','grow'}, dimensions={0} | all-to-all | bytes 262144 | tf_op jit(solution)/shard_map/all_to_all | solution.py:22
  107.4 0.0 collective-permute-done.8.t_other
  107.4 1.4 %copy-done.1 = f32[768,512]{1,0:T(8,128)S(1)} copy-done((f32[768,512]{1,0:T(8,128)S(1)}, f32[768,512]{1,0:T(8,128)}, u32[]{:S(2)}) %copy-start.1) | copy-done | bytes 1572888
  108.8 5.4 %shard_map.123 = f32[8,32,640]{2,1,0:T(8,128)S(1)} custom-call(f32[4,32,768]{2,1,0:T(8,128)S(1)} %all-to-all-done.got, f32[64,4,128]{2,1,0:T(4,128)S(1)} %all_to_all.20.total, f32[32,512]{1,0:T(8,128)S(1)} %get-tuple-element.16.mf, f32[768,512]{1,0:T(8,128)S(1)} %copy-done.1, f32[768,512]{1,0:T(8,128)S(1)} %collective-permute-done.8.t_other, ...), custom_call_target="tpu_custom_call" | custom-call | tf_op jit(solution)/shard_map/pallas_call | solution.py:38
  114.2 0.0 copy-start.2
  114.2 0.8 copy-done.2
  115.0 5.4 %all-to-all-start.3 = ((f32[8,32,640]{2,1,0:T(8,128)}), f32[8,32,640]{2,1,0:T(8,128)S(1)}, u32[]{:S(2)}, u32[]{:S(2)}) async-start(f32[8,32,640]{2,1,0:T(8,128)} %copy-done.2), calls=%async_computation.3 | async-start | bytes 1310720 | tf_op jit(solution)/shard_map/all_to_all | solution.py:22
  120.4 0.0 copy-done.4
  120.4 1.8 %convolution_bitcast_fusion.lead = f32[512,256]{1,0:T(8,128)S(1)} fusion(f32[512,256]{1,0:T(8,128)S(1)} %copy-done.4, f32[1,1,1,512,512]{4,3,2,1,0:T(8,128)S(1)} %copy-done), kind=kOutput, calls=%fused_computation.4 | convolution fusion | flops 805306368 | bytes 2097152 | tf_op jit(solution)/shard_map/dot_general | solution.py:16
  122.2 0.0 copy-done.6
  122.2 3.5 %convolution_multiply_fusion.link = f32[512,512]{1,0:T(8,128)S(1)} fusion(f32[1,1,1,512,512]{4,3,2,1,0:T(8,128)S(1)} %copy-done.6, f32[1,1,1,512,512]{4,3,2,1,0:T(8,128)S(1)} %copy-done, f32[]{:T(128)} %bitcast.6), kind=kOutput, calls=%fused_computation.1 | convolution fusion | flops 1610874880 | bytes 3145732 | tf_op jit(solution)/shard_map/dot_general | solution.py:16
  125.7 5.5 %all-to-all-done.3.back = f32[8,32,640]{2,1,0:T(8,128)S(1)} async-done(((f32[8,32,640]{2,1,0:T(8,128)}), f32[8,32,640]{2,1,0:T(8,128)S(1)}, u32[]{:S(2)}, u32[]{:S(2)}) %all-to-all-start.3) | async-done | bytes 655392 | tf_op jit(solution)/shard_map/all_to_all | solution.py:22
  131.2 1.5 %shard_map.124 = (f32[512,256]{1,0:T(8,128)}, f32[64,256]{1,0:T(8,128)}, f32[2,64,256]{2,1,0:T(8,128)}) custom-call(s32[1]{0:T(128)} %bitcast.me, f32[8,32,640]{2,1,0:T(8,128)S(1)} %all-to-all-done.3.back, f32[512,512]{1,0:T(8,128)S(1)} %convolution_multiply_fusion.link, f32[512,256]{1,0:T(8,128)S(1)} %convolution_bitcast_fusion.lead), custom_call_target="tpu_custom_call" | custom-call | tf_op jit(solution)/shard_map/pallas_call | solution.py:38
  (6 shorter events, 0.0 us)
Async XLA Ops:
  0.6 13.8 %copy-start = (f32[1,1,1,512,512]{4,3,2,1,0:T(8,128)S(1)}, f32[1,1,1,512,512]{4,3,2,1,0:T(8,128)}, u32[]{:S(2)}) copy-start(f32[1,1,1,512,512]{4,3,2,1,0:T(8,128)} %param.11) | copy-start | bytes 3145732
  2.8 17.7 %collective-permute-start.4 = (f32[192,512]{1,0:T(8,128)}, f32[192,512]{1,0:T(8,128)}, u32[]{:S(2)}, u32[]{:S(2)}) collective-permute-start(f32[192,512]{1,0:T(8,128)} %get-tuple-element.13), channel_id=1, source_target_pairs={{0,2},{2,4},{4,6},{6,0},{1,3},{3,5},{5,7},{7,1},{8,10},{10,12},{12... | collective-permute-start | bytes 1179656 | tf_op jit(solution)/shard_map/ppermute | solution.py:27
  6.7 14.8 %collective-permute-start.5 = (f32[192,512]{1,0:T(8,128)}, f32[192,512]{1,0:T(8,128)}, u32[]{:S(2)}, u32[]{:S(2)}) collective-permute-start(f32[192,512]{1,0:T(8,128)} %get-tuple-element.13), channel_id=1, source_target_pairs={{0,6},{2,0},{4,2},{6,4},{1,7},{3,1},{5,3},{7,5},{8,14},{10,8},{12,... | collective-permute-start | bytes 1179656 | tf_op jit(solution)/shard_map/ppermute | solution.py:27
  9.9 13.2 %collective-permute-start.6 = (f32[192,512]{1,0:T(8,128)}, f32[192,512]{1,0:T(8,128)}, u32[]{:S(2)}, u32[]{:S(2)}) collective-permute-start(f32[192,512]{1,0:T(8,128)} %get-tuple-element.13), channel_id=1, source_target_pairs={{0,4},{2,6},{4,0},{6,2},{1,5},{3,7},{5,1},{7,3},{8,12},{10,14},{12... | collective-permute-start | bytes 1179656 | tf_op jit(solution)/shard_map/ppermute | solution.py:27
  14.5 3.7 %copy-start.9 = (f32[1,1,64,256]{3,2,1,0:T(8,128)S(1)}, f32[1,1,64,256]{3,2,1,0:T(8,128)}, u32[]{:S(2)}) copy-start(f32[1,1,64,256]{3,2,1,0:T(8,128)} %param.14) | copy-start | bytes 196612
  16.5 17.8 %copy-start.3 = (f32[512,256]{1,0:T(8,128)}, f32[512,256]{1,0:T(8,128)S(1)}, u32[]{:S(2)}) copy-start(f32[512,256]{1,0:T(8,128)S(1)} %fusion.5) | copy-start | bytes 1572868
  19.3 15.0 %copy-start.5 = (f32[1,1,1,512,512]{4,3,2,1,0:T(8,128)S(1)}, f32[1,1,1,512,512]{4,3,2,1,0:T(8,128)}, u32[]{:S(2)}) copy-start(f32[1,1,1,512,512]{4,3,2,1,0:T(8,128)} %param.12) | copy-start | bytes 3145732
  19.3 15.0 %copy-start.7 = (f32[256,512]{1,0:T(8,128)S(1)}, f32[256,512]{1,0:T(8,128)}, u32[]{:S(2)}) copy-start(f32[256,512]{1,0:T(8,128)} %concatenate.18) | copy-start | bytes 1572868
  22.5 13.7 %copy-start.8 = (f32[256,128]{1,0:T(8,128)S(1)}, f32[256,128]{1,0:T(8,128)}, u32[]{:S(2)}) copy-start(f32[256,128]{1,0:T(8,128)} %get-tuple-element.24) | copy-start | bytes 393220
  24.2 32.3 %collective-permute-start.7 = (f32[768,512]{1,0:T(8,128)S(1)}, f32[768,512]{1,0:T(8,128)}, u32[]{:S(2)}, u32[]{:S(2)}) collective-permute-start(f32[768,512]{1,0:T(8,128)S(1)} %constant_dynamic-update-slice_fusion.mine), channel_id=1, source_target_pairs={{0,1},{1,0},{2,3},{3,2},{4,5},{5,4},{6,7},{7,6},{8,9},{9,8},{10,11... | collective-permute-start | bytes 4718600 | tf_op jit(solution)/shard_map/ppermute | solution.py:27
  37.1 3.9 %collective-permute-start = (f32[4,32,768]{2,1,0:T(8,128)}, f32[4,32,768]{2,1,0:T(8,128)}, u32[]{:S(2)}, u32[]{:S(2)}) collective-permute-start(f32[4,32,768]{2,1,0:T(8,128)} %dynamic-slice_bitcast_fusion), channel_id=1, source_target_pairs={{0,1},{1,0},{2,3},{3,2},{4,5},{5,4},{6,7},{7,6},{8,9},{9,8},{10,11... | collective-permute-start | bytes 1179656 | tf_op jit(solution)/shard_map/ppermute | solution.py:27
  42.8 13.6 %all-to-all-start = ((f32[4,32,768]{2,1,0:T(8,128)}), f32[4,32,768]{2,1,0:T(8,128)S(1)}, u32[]{:S(2)}, u32[]{:S(2)}) async-start(f32[4,32,768]{2,1,0:T(8,128)} %bitcast_add_fusion), calls=%async_computation | async-start | bytes 786432 | tf_op jit(solution)/shard_map/all_to_all | solution.py:22
  46.3 28.9 %collective-permute-start.1 = (f32[192,512]{1,0:T(8,128)}, f32[192,512]{1,0:T(8,128)}, u32[]{:S(2)}, u32[]{:S(2)}) collective-permute-start(f32[192,512]{1,0:T(8,128)} %get-tuple-element.12), channel_id=1, source_target_pairs={{0,2},{2,4},{4,6},{6,0},{1,3},{3,5},{5,7},{7,1},{8,10},{10,12},{12... | collective-permute-start | bytes 1179656 | tf_op jit(solution)/shard_map/ppermute | solution.py:27
  49.6 25.6 %collective-permute-start.2 = (f32[192,512]{1,0:T(8,128)}, f32[192,512]{1,0:T(8,128)}, u32[]{:S(2)}, u32[]{:S(2)}) collective-permute-start(f32[192,512]{1,0:T(8,128)} %get-tuple-element.12), channel_id=1, source_target_pairs={{0,6},{2,0},{4,2},{6,4},{1,7},{3,1},{5,3},{7,5},{8,14},{10,8},{12,... | collective-permute-start | bytes 1179656 | tf_op jit(solution)/shard_map/ppermute | solution.py:27
  52.8 22.4 %collective-permute-start.3 = (f32[192,512]{1,0:T(8,128)}, f32[192,512]{1,0:T(8,128)}, u32[]{:S(2)}, u32[]{:S(2)}) collective-permute-start(f32[192,512]{1,0:T(8,128)} %get-tuple-element.12), channel_id=1, source_target_pairs={{0,4},{2,6},{4,0},{6,2},{1,5},{3,7},{5,1},{7,3},{8,12},{10,14},{12... | collective-permute-start | bytes 1179656 | tf_op jit(solution)/shard_map/ppermute | solution.py:27
  59.7 26.9 %all-to-all-start.1 = ((f32[64,4,128]{2,1,0:T(4,128)}), f32[64,4,128]{2,1,0:T(4,128)S(1)}, u32[]{:S(2)}, u32[]{:S(2)}) async-start(f32[64,4,128]{2,1,0:T(4,128)} %get-tuple-element.14), calls=%async_computation.1 | async-start | bytes 262144 | tf_op jit(solution)/shard_map/all_to_all | solution.py:22
  86.7 20.7 %collective-permute-start.8 = (f32[768,512]{1,0:T(8,128)}, f32[768,512]{1,0:T(8,128)S(1)}, u32[]{:S(2)}, u32[]{:S(2)}) collective-permute-start(f32[768,512]{1,0:T(8,128)} %pad_maximum_fusion.t_mine), channel_id=1, source_target_pairs={{0,1},{1,0},{2,3},{3,2},{4,5},{5,4},{6,7},{7,6},{8,9},{9,8},{10,11... | collective-permute-start | bytes 4718600 | tf_op jit(solution)/shard_map/ppermute | solution.py:27
  107.4 1.4 %copy-start.1 = (f32[768,512]{1,0:T(8,128)S(1)}, f32[768,512]{1,0:T(8,128)}, u32[]{:S(2)}) copy-start(f32[768,512]{1,0:T(8,128)} %pad_maximum_fusion.t_mine) | copy-start | bytes 4718596
  114.2 0.8 copy-start.2
  115.0 5.4 %copy-start.4 = (f32[512,256]{1,0:T(8,128)S(1)}, f32[512,256]{1,0:T(8,128)}, u32[]{:S(2)}) copy-start(f32[512,256]{1,0:T(8,128)} %copy-done.3) | copy-start | bytes 1572868
  115.0 16.1 %all-to-all-start.3 = ((f32[8,32,640]{2,1,0:T(8,128)}), f32[8,32,640]{2,1,0:T(8,128)S(1)}, u32[]{:S(2)}, u32[]{:S(2)}) async-start(f32[8,32,640]{2,1,0:T(8,128)} %copy-done.2), calls=%async_computation.3 | async-start | bytes 1310720 | tf_op jit(solution)/shard_map/all_to_all | solution.py:22
  120.4 1.8 %copy-start.6 = (f32[1,1,1,512,512]{4,3,2,1,0:T(8,128)S(1)}, f32[1,1,1,512,512]{4,3,2,1,0:T(8,128)}, u32[]{:S(2)}) copy-start(f32[1,1,1,512,512]{4,3,2,1,0:T(8,128)} %param.12) | copy-start | bytes 3145732

commit v3 on v2

--- a/solution.py
+++ b/solution.py
@@ -37,7 +37,7 @@
     out_specs = jax.tree.map(lambda _: pl.BlockSpec(memory_space=pltpu.VMEM), outs)
     return pl.pallas_call(
         body, out_shape=outs, in_specs=specs, out_specs=out_specs, scratch_shapes=scratch,
-        compiler_params=pltpu.CompilerParams(vmem_limit_bytes=limit << 20),
+        compiler_params=pltpu.CompilerParams(vmem_limit_bytes=limit and limit << 20),
     )(*args)
 
 
@@ -68,6 +68,23 @@
         c.wait()
 
 
+def leaf_kernel(me, present, il, ll, rl, rm, rt, lead_in, sent):
+    n_g, cols, _ = sent.shape
+    block = il.shape[0]
+    share = block // n_g
+    kept = present[0].astype(jnp.float32)
+    fwd = dot3(split(rl[...].T), split(il[...]), 1, 1)
+    lead_in[...] = fwd
+    part = dot3(split(fwd), split(ll[...]), 1, 1) * kept
+    lane = lax.broadcasted_iota(jnp.int32, (1, block), 1)
+    own = (lane >= me[0] * share) & (lane < (me[0] + 1) * share)
+    part = jnp.where(own, jnp.concatenate([rm[...].T] * n_g, axis=1), 0.0) - part
+    tops = jnp.concatenate([rt[0].T, rt[1].T], axis=1)
+    for d in range(n_g):
+        sent[d, :, :block] = part[d * cols : (d + 1) * cols]
+        sent[d, :, block:] = tops[d * cols : (d + 1) * cols]
+
+
 def fill(high, low, blocks, part, share):
     n = 0
     for ref in blocks:
@@ -82,11 +99,11 @@
 
 def mid_kernel(got, mine, other, pieces, mf_out, high, low):
     blocks = [mine, other]
-    n_x, cols, _ = got.shape
+    n_g, cols, _ = got.shape
     block = other.shape[1]
-    share = mine.shape[0] // (3 * n_x)
+    share = block // n_g
     rhs = got[0, :, :block]
-    for c in range(1, n_x):
+    for c in range(1, n_g):
         rhs = rhs + got[c, :, :block]
     mf = dot3(split(rhs), fill(high.at[0], low.at[0], blocks, 0, share), 1, 1)
     mf_out[...] = mf
@@ -106,22 +123,22 @@
     out[...] = jnp.broadcast_to(total[None], out.shape)
 
 
-def top_kernel(got, total, mf, t_mine, t_other, mine, other, back, r, high, low, w_high, w_low):
-    n_x, cols, _ = got.shape
-    n_g, block = back.shape[0], other.shape[1]
-    share = block // n_g
-    two = 2 * share
+def top_kernel(got, total, mf, t0, t1, t2, t3, mine, other, back, r, high, low, w_high, w_low):
+    n_g, cols, _ = got.shape
+    block = other.shape[1]
+    share = block // n_g
     rows = total.shape[1]
     per = cols // rows
     for j in range(2 * block // 128):
         for i in range(per):
             r[i * rows : (i + 1) * rows, j * 128 : (j + 1) * 128] = total[j * per + i]
     for k in range(2):
-        for x in range(n_x):
-            at = k * block + x * two
-            r[:, at : at + two] = got[x, :, block + k * two : block + (k + 1) * two] - r[:, at : at + two]
+        rt = jnp.concatenate(
+            [got[c, :, block + k * share : block + (k + 1) * share] for c in range(n_g)], axis=1
+        )
+        r[:, k * block : (k + 1) * block] = rt - r[:, k * block : (k + 1) * block]
     it0, it1, ut = (
-        fill(high.at[p], low.at[p], [t_mine, t_other], p, share) for p in range(3)
+        fill(high.at[p], low.at[p], [t0, t1, t2, t3], p, share) for p in range(3)
     )
     f0 = dot3(split(r[:, :block]), it0, 1, 1)
     f1 = dot3(split(r[:, block:] - dot3(split(f0), ut, 1, 0)), it1, 1, 1)
@@ -164,12 +181,12 @@
     inverse_top,
     upper_top,
 ):
-    n_x, n_c, n_lg = lax.axis_size(GX), lax.axis_size(GC), lax.axis_size(LG)
-    n_g = n_x * n_c
+    n_lg = lax.axis_size(LG)
+    n_g = lax.axis_size(GCOL)
     block, nrhs = right_leaf.shape[-2:]
     share = block // n_g
     cols = nrhs // n_g
-    me, core = lax.axis_index(GCOL), lax.axis_index(GC)
+    me = lax.axis_index(GCOL)
     il, ll, rl = inverse_leaf[0, 0, 0], lower_leaf[0, 0, 0], right_leaf[0, 0, 0]
     kept = present[0, 0, 0].astype(jnp.float32)
 
@@ -182,27 +199,27 @@
         out_specs=(vmem_spec, vmem_spec),
         scratch_shapes=[pltpu.SemaphoreType.DMA((4,))],
         name="pack",
-    )(inverse_middle[0, 0], upper_middle.reshape(2 * share, block), inverse_top.reshape(2 * share, block), upper_top[0])
+    )(
+        inverse_middle[0, 0],
+        upper_middle.reshape(2 * share, block),
+        inverse_top.reshape(2 * share, block),
+        upper_top[0],
+    )
     ws = [w, shift(w, GX, 1), shift(w, GX, -1), shift(w, GX, 2)]
-    leaf_fwd = dot(il, rl, 1, 0)
-    part = dot(leaf_fwd, ll, 0, 1) * kept
-    lane = lax.broadcasted_iota(jnp.int32, (1, block), 1)
-    own = (lane >= me * share) & (lane < (me + 1) * share)
-    rm = right_middle[0, 0].T
-    part = jnp.where(own, jnp.concatenate([rm] * n_g, axis=1), 0.0) - part
-    first = lax.broadcasted_iota(jnp.int32, (1, n_c * share), 1) // share == core
-    rts = [jnp.where(first, jnp.concatenate([right_top[k].T] * n_c, axis=1), 0.0) for k in range(2)]
-    sent = jnp.concatenate([part, *rts], axis=1).reshape(n_x, n_c, cols, -1)
-    keep = lax.dynamic_index_in_dim(sent, core, 1, keepdims=False)
-    give = lax.dynamic_index_in_dim(sent, 1 - core, 1, keepdims=False)
-    take = shift(give, GC, 1)
-    keep = keep + take
-    lead = dot(il, leaf_fwd, 0, 0)
+    t = jnp.concatenate([t, shift(t, GC, 1)], axis=0)
+    leaf_fwd, sent = kernel_call(
+        leaf_kernel,
+        (f32(nrhs, block), f32(n_g, cols, block + 2 * share)),
+        me.reshape(1).astype(jnp.int32), present.reshape(1), il, ll, rl, right_middle[0, 0], right_top,
+        scalars=2, limit=None,
+    )
+    lead = dot(il, leaf_fwd, 0, 1)
     link = dot(il, ll, 0, 1) * kept
-    got = swap(keep, GX)
+    got = swap(sent, GCOL)
     mine = jnp.concatenate(ws, axis=0)
     other = shift(mine, GC, 1)
-    ts = [t, shift(t, GX, 1), shift(t, GX, -1), shift(t, GX, 2)]
+    t2 = shift(t, GX, 2)
+    t1, t3 = shift(t, GX, 1), shift(t, GX, -1)
     halves = pltpu.VMEM((3, block, block), jnp.bfloat16)
     pieces, mf = kernel_call(
         mid_kernel,
@@ -210,12 +227,10 @@
         got, mine, other, scratch=[halves, halves],
     )
     arrived = swap(pieces, LG)
-    t_mine, arrived = lax.optimization_barrier((jnp.concatenate(ts, axis=0), arrived))
-    t_other = shift(t_mine, GC, 1)
     total = kernel_call(sum_kernel, pieces, arrived)
     total = swap(total, LG)
     back = kernel_call(
-        top_kernel, f32(n_g, cols, block + 2 * share), got, total, mf, t_mine, t_other, mine, other,
+        top_kernel, f32(n_g, cols, block + 2 * share), got, total, mf, t, t1, t2, t3, mine, other,
         scratch=[pltpu.VMEM((cols, 2 * block), jnp.float32), halves, halves, halves, halves],
     )
     back = swap(back, GCOL)

time: 134 us -> 129 us (0.963)
  starting transfers between devices: 62 us -> 48.4 us
  blocking collectives: 15.7 us -> 27 us
  waiting for transfers between devices: 17 us -> 24.4 us
  other arithmetic: 5.26 us -> 0 us
  local copies, waits for them, and re-layouts: 9.44 us -> 4.54 us
  Pallas kernels: 12.4 us -> 16.3 us
  matrix products: 9.23 us -> 6.42 us
    all_to_all x1, blocking collectives: 15.7 us -> 27 us  [swap(): return lax.all_to_all(x, axis, split_axis=0, concat_axis=0, tiled=True)]
    all_to_all x3, starting transfers between devices: 24.2 us -> 16.9 us  [swap(): return lax.all_to_all(x, axis, split_axis=0, concat_axis=0, tiled=True)]
    ppermute x9 -> x8, starting transfers between devices: 37.7 us -> 31.5 us  [shift(): return lax.ppermute(x, axis, [(s, (s + step) % n) for s in range(n)])]
    ppermute x9 -> x8, waiting for transfers between devices: 2.66 us -> 8.4 us  [shift(): return lax.ppermute(x, axis, [(s, (s + step) % n) for s in range(n)])]
    pallas_call x4 -> x5, Pallas kernels: 10.3 us -> 14.3 us  [kernel_call(): pl.pallas_call(body, out_shape=outs, in_specs=specs, out_specs=out_specs,...]
    unnamed x26 -> x12, local copies, waits for them, and re-layouts: 5.74 us -> 2.74 us
    dot_general x4 -> x2, matrix products: 9.23 us -> 6.42 us  [dot(): lax.dot_general(a, b, (((ca,), (cb,)), ((), ())), precision=PRECISE, pref...]
    concatenate x2 -> x0, other arithmetic: 2.67 us -> none  [the longest x1 2.61 us: local(): jnp.concatenate(ts, axis=0)]
  transfers between devices with their start and end apart: 12 -> 11, of which waited for: 4 -> 4; matrix products, arithmetic and copies ran while one was open for 16% -> 8% of each run, Pallas kernels for 3% -> 5%
where the time goes in v3:
time: 129 us
  starting transfers between devices  48.4 us (38%)
  blocking collectives  27 us (21%)
  waiting for transfers between devices  24.4 us (19%)
  Pallas kernels  16.3 us (13%)
  matrix products  6.42 us (5%)
  local copies, waits for them, and re-layouts  4.54 us (4%)
  between operations  1.5 us (1%)
    ppermute x8, starting transfers between devices, shift(): return lax.ppermute(x, axis, [(s, (s + step) % n) for s in range(n)])  31.5 us
    all_to_all x1, blocking collectives, swap(): return lax.all_to_all(x, axis, split_axis=0, concat_axis=0, tiled=True)  27 us
    all_to_all x3, starting transfers between devices, swap(): return lax.all_to_all(x, axis, split_axis=0, concat_axis=0, tiled=True)  16.9 us
    all_to_all x3, waiting for transfers between devices, swap(): return lax.all_to_all(x, axis, split_axis=0, concat_axis=0, tiled=True)  16 us
    pallas_call x5, Pallas kernels, kernel_call(): pl.pallas_call(body, out_shape=outs, in_specs=specs, out_specs=out_specs,...  14.3 us
    ppermute x8, waiting for transfers between devices, shift(): return lax.ppermute(x, axis, [(s, (s + step) % n) for s in range(n)])  8.4 us
    dot_general x2, matrix products, dot(): lax.dot_general(a, b, (((ca,), (cb,)), ((), ())), precision=PRECISE, pref...  6.42 us
    unnamed x12, local copies, waits for them, and re-layouts  2.74 us
  transfers between devices with their start and end apart: 11, of which 4 were waited for; matrix products, arithmetic and copies ran while one was open for 8% of the time, Pallas kernels for 5%

profile of v3, /device:TPU:1, one launch (start us, length us, event | category | flops | bytes accessed | tf_op | source)
XLA Modules:
  0.0 128.5 jit_solution(14461493613579905222)
XLA Ops:
  0.6 2.0 %pack.1 = (f32[192,512]{1,0:T(8,128)}, f32[192,512]{1,0:T(8,128)}) custom-call(f32[64,512]{1,0:T(8,128)} %bitcast.28, f32[128,512]{1,0:T(8,128)} %bitcast.26, f32[128,512]{1,0:T(8,128)} %bitcast.27, f32[64,512]{1,0:T(8,128)} %bitcast.29), custom_call_target="tpu_custom_call" | custom-call | tf_op jit(solution)/shard_map/pack/pallas_call | solution.py:195
  2.7 0.0 copy-start.3
  2.7 4.1 %collective-permute-start = (f32[192,512]{1,0:T(8,128)}, f32[192,512]{1,0:T(8,128)S(1)}, u32[]{:S(2)}, u32[]{:S(2)}) collective-permute-start(f32[192,512]{1,0:T(8,128)} %get-tuple-element.13), channel_id=1, source_target_pairs={{0,2},{2,4},{4,6},{6,0},{1,3},{3,5},{5,7},{7,1},{8,10},{10,12},{12... | collective-permute-start | bytes 1179656 | tf_op jit(solution)/shard_map/ppermute | solution.py:27
  6.8 3.2 %collective-permute-start.1 = (f32[192,512]{1,0:T(8,128)}, f32[192,512]{1,0:T(8,128)S(1)}, u32[]{:S(2)}, u32[]{:S(2)}) collective-permute-start(f32[192,512]{1,0:T(8,128)} %get-tuple-element.13), channel_id=1, source_target_pairs={{0,6},{2,0},{4,2},{6,4},{1,7},{3,1},{5,3},{7,5},{8,14},{10,8},{12,... | collective-permute-start | bytes 1179656 | tf_op jit(solution)/shard_map/ppermute | solution.py:27
  10.0 3.6 %collective-permute-start.2 = (f32[192,512]{1,0:T(8,128)}, f32[192,512]{1,0:T(8,128)S(1)}, u32[]{:S(2)}, u32[]{:S(2)}) collective-permute-start(f32[192,512]{1,0:T(8,128)} %get-tuple-element.13), channel_id=1, source_target_pairs={{0,4},{2,6},{4,0},{6,2},{1,5},{3,7},{5,1},{7,3},{8,12},{10,14},{12... | collective-permute-start | bytes 1179656 | tf_op jit(solution)/shard_map/ppermute | solution.py:27
  13.6 1.0 constant_dynamic-update-slice_fusion.3
  14.6 0.0 collective-permute-done
  14.7 0.8 collective-permute-done.1
  15.5 7.6 %collective-permute-done.2 = f32[192,512]{1,0:T(8,128)S(1)} collective-permute-done((f32[192,512]{1,0:T(8,128)}, f32[192,512]{1,0:T(8,128)S(1)}, u32[]{:S(2)}, u32[]{:S(2)}) %collective-permute-start.2) | collective-permute-done | bytes 393248 | tf_op jit(solution)/shard_map/ppermute | solution.py:27
  23.1 8.1 %collective-permute-start.3 = (f32[768,512]{1,0:T(8,128)S(1)}, f32[768,512]{1,0:T(8,128)S(1)}, u32[]{:S(2)}, u32[]{:S(2)}) collective-permute-start(f32[768,512]{1,0:T(8,128)S(1)} %constant_dynamic-update-slice_fusion.mine), channel_id=1, source_target_pairs={{0,1},{1,0},{2,3},{3,2},{4,5},{5,4},{6,7},{7,6},{8,9},{9,8},{10,11... | collective-permute-start | bytes 4718600 | tf_op jit(solution)/shard_map/ppermute | solution.py:27
  31.2 0.0 copy-done.3
  31.2 1.9 %collective-permute-start.4 = (f32[192,512]{1,0:T(8,128)S(1)}, f32[192,512]{1,0:T(8,128)}, u32[]{:S(2)}, u32[]{:S(2)}) collective-permute-start(f32[192,512]{1,0:T(8,128)S(1)} %copy-done.3), channel_id=1, source_target_pairs={{0,1},{1,0},{2,3},{3,2},{4,5},{5,4},{6,7},{7,6},{8,9},{9,8},{10,11... | collective-permute-start | bytes 1179656 | tf_op jit(solution)/shard_map/ppermute | solution.py:27
  33.8 3.7 %shard_map.121 = (f32[256,512]{1,0:T(8,128)}, f32[8,32,640]{2,1,0:T(8,128)}) custom-call(s32[1]{0:T(128)} %bitcast.me, s32[1]{0:T(128)} %bitcast.22.present, f32[512,512]{1,0:T(8,128)} %bitcast.23, f32[512,512]{1,0:T(8,128)} %bitcast.24, f32[512,256]{1,0:T(8,128)} %bitcast.25, f32[64,256]{1,0:T(8,128)} %bitcast.30, f32[2,64,256]{2,1,0:T(8,128)} %rt.1), custom_call_target="tpu_custom_call" | custom-call | tf_op jit(solution)/shard_map/pallas_call | solution.py:38
  37.5 5.0 %all-to-all-start = ((f32[8,32,640]{2,1,0:T(8,128)}), f32[8,32,640]{2,1,0:T(8,128)}, u32[]{:S(2)}, u32[]{:S(2)}) async-start(f32[8,32,640]{2,1,0:T(8,128)} %get-tuple-element.12), calls=%async_computation | async-start | bytes 1310720 | tf_op jit(solution)/shard_map/all_to_all | solution.py:22
  42.5 0.8 constant_dynamic-update-slice_fusion.5
  43.3 0.0 collective-permute-done.4
  43.3 1.8 %constant_dynamic-update-slice_fusion.4.t0 = f32[384,512]{1,0:T(8,128)} fusion(f32[384,512]{1,0:T(8,128)} %constant_dynamic-update-slice_fusion.5, f32[192,512]{1,0:T(8,128)} %collective-permute-done.4), kind=kLoop, calls=%fused_computation.6 | loop fusion | bytes 786432 | tf_op jit(solution)/shard_map/concatenate | solution.py:209
  45.1 3.2 %collective-permute-start.5 = (f32[384,512]{1,0:T(8,128)}, f32[384,512]{1,0:T(8,128)}, u32[]{:S(2)}, u32[]{:S(2)}) collective-permute-start(f32[384,512]{1,0:T(8,128)} %constant_dynamic-update-slice_fusion.4.t0), channel_id=1, source_target_pairs={{0,2},{2,4},{4,6},{6,0},{1,3},{3,5},{5,7},{7,1},{8,10},{10,12},{12... | collective-permute-start | bytes 2359304 | tf_op jit(solution)/shard_map/ppermute | solution.py:27
  48.3 4.3 %collective-permute-start.6 = (f32[384,512]{1,0:T(8,128)}, f32[384,512]{1,0:T(8,128)}, u32[]{:S(2)}, u32[]{:S(2)}) collective-permute-start(f32[384,512]{1,0:T(8,128)} %constant_dynamic-update-slice_fusion.4.t0), channel_id=1, source_target_pairs={{0,4},{2,6},{4,0},{6,2},{1,5},{3,7},{5,1},{7,3},{8,12},{10,14},{12... | collective-permute-start | bytes 2359304 | tf_op jit(solution)/shard_map/ppermute | solution.py:27
  52.6 3.1 %collective-permute-start.7 = (f32[384,512]{1,0:T(8,128)}, f32[384,512]{1,0:T(8,128)}, u32[]{:S(2)}, u32[]{:S(2)}) collective-permute-start(f32[384,512]{1,0:T(8,128)} %constant_dynamic-update-slice_fusion.4.t0), channel_id=1, source_target_pairs={{0,6},{2,0},{4,2},{6,4},{1,7},{3,1},{5,3},{7,5},{8,14},{10,8},{12,... | collective-permute-start | bytes 2359304 | tf_op jit(solution)/shard_map/ppermute | solution.py:27
  55.7 0.0 all-to-all-done.got
  55.7 0.0 collective-permute-done.3.other
  55.7 2.3 %shard_map.122 = (f32[64,4,128]{2,1,0:T(4,128)S(1)}, f32[32,512]{1,0:T(8,128)S(1)}) custom-call(f32[8,32,640]{2,1,0:T(8,128)} %all-to-all-done.got, f32[768,512]{1,0:T(8,128)S(1)} %constant_dynamic-update-slice_fusion.mine, f32[768,512]{1,0:T(8,128)S(1)} %collective-permute-done.3.other), custom_call_target="tpu_custom_call" | custom-call | tf_op jit(solution)/shard_map/pallas_call | solution.py:38
  58.1 27.0 %all_to_all.20.pieces = f32[64,4,128]{2,1,0:T(4,128)S(1)} all-to-all(f32[64,4,128]{2,1,0:T(4,128)S(1)} %get-tuple-element.14), channel_id=1, replica_groups=mesh['leaf'=8,'grow'=8,'gcol_0'=4,'gcol_1'=2] {'leaf','grow'}, dimensions={0} | all-to-all | bytes 262144 | tf_op jit(solution)/shard_map/all_to_all | solution.py:22
  85.0 0.7 shard_map.123
  85.8 4.6 %all-to-all-start.2 = ((f32[64,4,128]{2,1,0:T(4,128)}), f32[64,4,128]{2,1,0:T(4,128)S(1)}, u32[]{:S(2)}, u32[]{:S(2)}) async-start(f32[64,4,128]{2,1,0:T(4,128)} %shard_map.123), calls=%async_computation.2 | async-start | bytes 262144 | tf_op jit(solution)/shard_map/all_to_all | solution.py:22
  90.4 0.0 collective-permute-done.5.t1
  90.4 0.0 collective-permute-done.6.t2
  90.4 0.0 collective-permute-done.7.t3
  90.4 11.7 %all-to-all-done.2.total = f32[64,4,128]{2,1,0:T(4,128)S(1)} async-done(((f32[64,4,128]{2,1,0:T(4,128)}), f32[64,4,128]{2,1,0:T(4,128)S(1)}, u32[]{:S(2)}, u32[]{:S(2)}) %all-to-all-start.2) | async-done | bytes 131104 | tf_op jit(solution)/shard_map/all_to_all | solution.py:22
  102.1 6.0 %shard_map.124 = f32[8,32,640]{2,1,0:T(8,128)S(1)} custom-call(f32[8,32,640]{2,1,0:T(8,128)} %all-to-all-done.got, f32[64,4,128]{2,1,0:T(4,128)S(1)} %all-to-all-done.2.total, f32[32,512]{1,0:T(8,128)S(1)} %get-tuple-element.15.mf, f32[384,512]{1,0:T(8,128)} %constant_dynamic-update-slice_fusion.4.t0, f32[384,512]{1,0:T(8,128)} %collective-permute-done.5.t1, ...), custom_call_target="tpu_custom_call" | custom-call | tf_op jit(solution)/shard_map/pallas_call | solution.py:38
  108.2 0.0 copy-start
  108.2 0.8 copy-done
  109.0 0.0 copy-start.1
  109.0 7.3 %all-to-all-start.3 = ((f32[8,32,640]{2,1,0:T(8,128)}), f32[8,32,640]{2,1,0:T(8,128)S(1)}, u32[]{:S(2)}, u32[]{:S(2)}) async-start(f32[8,32,640]{2,1,0:T(8,128)} %copy-done), calls=%async_computation.3 | async-start | bytes 1310720 | tf_op jit(solution)/shard_map/all_to_all | solution.py:22
  116.3 0.0 copy-start.2
  116.3 0.0 copy-done.1
  116.3 2.9 %convolution_bitcast_fusion.lead = f32[512,256]{1,0:T(8,128)S(1)} fusion(f32[256,512]{1,0:T(8,128)} %get-tuple-element.17, f32[1,1,1,512,512]{4,3,2,1,0:T(8,128)S(1)} %copy-done.1), kind=kOutput, calls=%fused_computation.1 | convolution fusion | flops 805306368 | bytes 2097152 | tf_op jit(solution)/shard_map/dot_general | solution.py:16
  119.2 0.0 copy-done.2
  119.2 3.5 %convolution_multiply_fusion.link = f32[512,512]{1,0:T(8,128)S(1)} fusion(f32[]{:T(128)} %bitcast.10, f32[1,1,1,512,512]{4,3,2,1,0:T(8,128)S(1)} %copy-done.2, f32[1,1,1,512,512]{4,3,2,1,0:T(8,128)S(1)} %copy-done.1), kind=kOutput, calls=%fused_computation | convolution fusion | flops 1610874880 | bytes 3145732 | tf_op jit(solution)/shard_map/dot_general | solution.py:16
  122.7 4.3 %all-to-all-done.3.back = f32[8,32,640]{2,1,0:T(8,128)S(1)} async-done(((f32[8,32,640]{2,1,0:T(8,128)}), f32[8,32,640]{2,1,0:T(8,128)S(1)}, u32[]{:S(2)}, u32[]{:S(2)}) %all-to-all-start.3) | async-done | bytes 655392 | tf_op jit(solution)/shard_map/all_to_all | solution.py:22
  127.1 1.5 %shard_map.125 = (f32[512,256]{1,0:T(8,128)}, f32[64,256]{1,0:T(8,128)}, f32[2,64,256]{2,1,0:T(8,128)}) custom-call(s32[1]{0:T(128)} %bitcast.me, f32[8,32,640]{2,1,0:T(8,128)S(1)} %all-to-all-done.3.back, f32[512,512]{1,0:T(8,128)S(1)} %convolution_multiply_fusion.link, f32[512,256]{1,0:T(8,128)S(1)} %convolution_bitcast_fusion.lead), custom_call_target="tpu_custom_call" | custom-call | tf_op jit(solution)/shard_map/pallas_call | solution.py:38
  (3 shorter events, 0.1 us)
Async XLA Ops:
  2.7 28.5 %copy-start.3 = (f32[192,512]{1,0:T(8,128)S(1)}, f32[192,512]{1,0:T(8,128)}, u32[]{:S(2)}) copy-start(f32[192,512]{1,0:T(8,128)} %get-tuple-element.16) | copy-start | bytes 1179652
  2.7 11.9 %collective-permute-start = (f32[192,512]{1,0:T(8,128)}, f32[192,512]{1,0:T(8,128)S(1)}, u32[]{:S(2)}, u32[]{:S(2)}) collective-permute-start(f32[192,512]{1,0:T(8,128)} %get-tuple-element.13), channel_id=1, source_target_pairs={{0,2},{2,4},{4,6},{6,0},{1,3},{3,5},{5,7},{7,1},{8,10},{10,12},{12... | collective-permute-start | bytes 1179656 | tf_op jit(solution)/shard_map/ppermute | solution.py:27
  6.8 8.7 %collective-permute-start.1 = (f32[192,512]{1,0:T(8,128)}, f32[192,512]{1,0:T(8,128)S(1)}, u32[]{:S(2)}, u32[]{:S(2)}) collective-permute-start(f32[192,512]{1,0:T(8,128)} %get-tuple-element.13), channel_id=1, source_target_pairs={{0,6},{2,0},{4,2},{6,4},{1,7},{3,1},{5,3},{7,5},{8,14},{10,8},{12,... | collective-permute-start | bytes 1179656 | tf_op jit(solution)/shard_map/ppermute | solution.py:27
  10.0 13.1 %collective-permute-start.2 = (f32[192,512]{1,0:T(8,128)}, f32[192,512]{1,0:T(8,128)S(1)}, u32[]{:S(2)}, u32[]{:S(2)}) collective-permute-start(f32[192,512]{1,0:T(8,128)} %get-tuple-element.13), channel_id=1, source_target_pairs={{0,4},{2,6},{4,0},{6,2},{1,5},{3,7},{5,1},{7,3},{8,12},{10,14},{12... | collective-permute-start | bytes 1179656 | tf_op jit(solution)/shard_map/ppermute | solution.py:27
  23.1 32.6 %collective-permute-start.3 = (f32[768,512]{1,0:T(8,128)S(1)}, f32[768,512]{1,0:T(8,128)S(1)}, u32[]{:S(2)}, u32[]{:S(2)}) collective-permute-start(f32[768,512]{1,0:T(8,128)S(1)} %constant_dynamic-update-slice_fusion.mine), channel_id=1, source_target_pairs={{0,1},{1,0},{2,3},{3,2},{4,5},{5,4},{6,7},{7,6},{8,9},{9,8},{10,11... | collective-permute-start | bytes 4718600 | tf_op jit(solution)/shard_map/ppermute | solution.py:27
  31.2 12.0 %collective-permute-start.4 = (f32[192,512]{1,0:T(8,128)S(1)}, f32[192,512]{1,0:T(8,128)}, u32[]{:S(2)}, u32[]{:S(2)}) collective-permute-start(f32[192,512]{1,0:T(8,128)S(1)} %copy-done.3), channel_id=1, source_target_pairs={{0,1},{1,0},{2,3},{3,2},{4,5},{5,4},{6,7},{7,6},{8,9},{9,8},{10,11... | collective-permute-start | bytes 1179656 | tf_op jit(solution)/shard_map/ppermute | solution.py:27
  37.5 18.2 %all-to-all-start = ((f32[8,32,640]{2,1,0:T(8,128)}), f32[8,32,640]{2,1,0:T(8,128)}, u32[]{:S(2)}, u32[]{:S(2)}) async-start(f32[8,32,640]{2,1,0:T(8,128)} %get-tuple-element.12), calls=%async_computation | async-start | bytes 1310720 | tf_op jit(solution)/shard_map/all_to_all | solution.py:22
  45.1 45.3 %collective-permute-start.5 = (f32[384,512]{1,0:T(8,128)}, f32[384,512]{1,0:T(8,128)}, u32[]{:S(2)}, u32[]{:S(2)}) collective-permute-start(f32[384,512]{1,0:T(8,128)} %constant_dynamic-update-slice_fusion.4.t0), channel_id=1, source_target_pairs={{0,2},{2,4},{4,6},{6,0},{1,3},{3,5},{5,7},{7,1},{8,10},{10,12},{12... | collective-permute-start | bytes 2359304 | tf_op jit(solution)/shard_map/ppermute | solution.py:27
  48.3 42.1 %collective-permute-start.6 = (f32[384,512]{1,0:T(8,128)}, f32[384,512]{1,0:T(8,128)}, u32[]{:S(2)}, u32[]{:S(2)}) collective-permute-start(f32[384,512]{1,0:T(8,128)} %constant_dynamic-update-slice_fusion.4.t0), channel_id=1, source_target_pairs={{0,4},{2,6},{4,0},{6,2},{1,5},{3,7},{5,1},{7,3},{8,12},{10,14},{12... | collective-permute-start | bytes 2359304 | tf_op jit(solution)/shard_map/ppermute | solution.py:27
  52.6 37.8 %collective-permute-start.7 = (f32[384,512]{1,0:T(8,128)}, f32[384,512]{1,0:T(8,128)}, u32[]{:S(2)}, u32[]{:S(2)}) collective-permute-start(f32[384,512]{1,0:T(8,128)} %constant_dynamic-update-slice_fusion.4.t0), channel_id=1, source_target_pairs={{0,6},{2,0},{4,2},{6,4},{1,7},{3,1},{5,3},{7,5},{8,14},{10,8},{12,... | collective-permute-start | bytes 2359304 | tf_op jit(solution)/shard_map/ppermute | solution.py:27
  85.8 16.3 %all-to-all-start.2 = ((f32[64,4,128]{2,1,0:T(4,128)}), f32[64,4,128]{2,1,0:T(4,128)S(1)}, u32[]{:S(2)}, u32[]{:S(2)}) async-start(f32[64,4,128]{2,1,0:T(4,128)} %shard_map.123), calls=%async_computation.2 | async-start | bytes 262144 | tf_op jit(solution)/shard_map/all_to_all | solution.py:22
  108.2 0.9 copy-start
  109.0 7.3 %copy-start.1 = (f32[1,1,1,512,512]{4,3,2,1,0:T(8,128)S(1)}, f32[1,1,1,512,512]{4,3,2,1,0:T(8,128)}, u32[]{:S(2)}) copy-start(f32[1,1,1,512,512]{4,3,2,1,0:T(8,128)} %param.11) | copy-start | bytes 3145732
  109.0 18.1 %all-to-all-start.3 = ((f32[8,32,640]{2,1,0:T(8,128)}), f32[8,32,640]{2,1,0:T(8,128)S(1)}, u32[]{:S(2)}, u32[]{:S(2)}) async-start(f32[8,32,640]{2,1,0:T(8,128)} %copy-done), calls=%async_computation.3 | async-start | bytes 1310720 | tf_op jit(solution)/shard_map/all_to_all | solution.py:22
  116.3 3.0 %copy-start.2 = (f32[1,1,1,512,512]{4,3,2,1,0:T(8,128)S(1)}, f32[1,1,1,512,512]{4,3,2,1,0:T(8,128)}, u32[]{:S(2)}) copy-start(f32[1,1,1,512,512]{4,3,2,1,0:T(8,128)} %param.12) | copy-start | bytes 3145732

commit v4 on v3

--- a/solution.py
+++ b/solution.py
@@ -53,6 +53,10 @@
         )
 
     (ah, al), (bh, bl) = a, b
+    m = ah.shape[0]
+    if ca == 1 and m < 128:
+        both = one(jnp.concatenate([ah, al], axis=0), bh)
+        return both[:m] + (one(ah, bl) + both[m:])
     return one(ah, bh) + (one(ah, bl) + one(al, bh))
 
 
@@ -123,7 +127,7 @@
     out[...] = jnp.broadcast_to(total[None], out.shape)
 
 
-def top_kernel(got, total, mf, t0, t1, t2, t3, mine, other, back, r, high, low, w_high, w_low):
+def top_kernel(late, got, total, mf, t0, t1, t2, t3, mine, other, back, r, high, low, w_high, w_low):
     n_g, cols, _ = got.shape
     block = other.shape[1]
     share = block // n_g
@@ -154,13 +158,14 @@
         back[d, :, block + share :] = s1[:, d * share : (d + 1) * share]
 
 
-def end_kernel(me, back, link, lead, leaf_out, mid_out, top_out):
+def end_kernel(me, present, back, link, lead, leaf_out, mid_out, top_out):
     n_g, cols, _ = back.shape
     block = link.shape[0]
     share = block // n_g
     both = back[...].reshape(n_g * cols, back.shape[2])
     sm = both[:, :block]
-    leaf_out[...] = lead[...] - dot3(split(link[...]), split(sm), 1, 1)
+    kept = present[0].astype(jnp.float32)
+    leaf_out[...] = lead[...] - kept * dot3(split(link[...]), split(sm), 1, 1)
     mine = jnp.zeros((n_g * cols, share), jnp.float32)
     for c in range(n_g):
         mine = jnp.where(me[0] == c, sm[:, c * share : (c + 1) * share], mine)
@@ -188,7 +193,6 @@
     cols = nrhs // n_g
     me = lax.axis_index(GCOL)
     il, ll, rl = inverse_leaf[0, 0, 0], lower_leaf[0, 0, 0], right_leaf[0, 0, 0]
-    kept = present[0, 0, 0].astype(jnp.float32)
 
     any_spec = pl.BlockSpec(memory_space=pl.ANY)
     vmem_spec = pl.BlockSpec(memory_space=pltpu.VMEM)
@@ -199,12 +203,7 @@
         out_specs=(vmem_spec, vmem_spec),
         scratch_shapes=[pltpu.SemaphoreType.DMA((4,))],
         name="pack",
-    )(
-        inverse_middle[0, 0],
-        upper_middle.reshape(2 * share, block),
-        inverse_top.reshape(2 * share, block),
-        upper_top[0],
-    )
+    )(inverse_middle[0, 0], upper_middle.reshape(2 * share, block), inverse_top.reshape(2 * share, block), upper_top[0])
     ws = [w, shift(w, GX, 1), shift(w, GX, -1), shift(w, GX, 2)]
     t = jnp.concatenate([t, shift(t, GC, 1)], axis=0)
     leaf_fwd, sent = kernel_call(
@@ -214,7 +213,7 @@
         scalars=2, limit=None,
     )
     lead = dot(il, leaf_fwd, 0, 1)
-    link = dot(il, ll, 0, 1) * kept
+    link = dot(il, ll, 0, 1)
     got = swap(sent, GCOL)
     mine = jnp.concatenate(ws, axis=0)
     other = shift(mine, GC, 1)
@@ -229,15 +228,16 @@
     arrived = swap(pieces, LG)
     total = kernel_call(sum_kernel, pieces, arrived)
     total = swap(total, LG)
+    late = lax.slice(total, (0, 0, 0), (1, 1, 128))
     back = kernel_call(
-        top_kernel, f32(n_g, cols, block + 2 * share), got, total, mf, t, t1, t2, t3, mine, other,
+        top_kernel, f32(n_g, cols, block + 2 * share), late, got, total, mf, t, t1, t2, t3, mine, other,
         scratch=[pltpu.VMEM((cols, 2 * block), jnp.float32), halves, halves, halves, halves],
     )
     back = swap(back, GCOL)
     leaf_back, solve_middle, solve_top = kernel_call(
         end_kernel,
         (f32(block, nrhs), f32(share, nrhs), f32(2, share, nrhs)),
-        me.reshape(1).astype(jnp.int32), back, link, lead, scalars=1,
+        me.reshape(1).astype(jnp.int32), present.reshape(1), back, link, lead, scalars=2,
     )
     return (leaf_back[None, None, None], solve_middle[None, None], solve_top)
 

time: 129 us -> 126 us (0.977)
  blocking collectives: 27 us -> 42.5 us
  waiting for transfers between devices: 24.4 us -> 12.7 us
  starting transfers between devices: 48.4 us -> 43.8 us
  Pallas kernels: 16.3 us -> 14.2 us
    all_to_all x1 -> x2, blocking collectives: 27 us -> 42.5 us  [swap(): return lax.all_to_all(x, axis, split_axis=0, concat_axis=0, tiled=True)]
    all_to_all x3 -> x2, waiting for transfers between devices: 16 us -> 4.34 us  [swap(): return lax.all_to_all(x, axis, split_axis=0, concat_axis=0, tiled=True)]
    all_to_all x3 -> x2, starting transfers between devices: 16.9 us -> 12.2 us  [swap(): return lax.all_to_all(x, axis, split_axis=0, concat_axis=0, tiled=True)]
    pallas_call x5, Pallas kernels: 14.3 us -> 12.1 us  [kernel_call(): pl.pallas_call(body, out_shape=outs, in_specs=specs, out_specs=out_specs,...]
  transfers between devices with their start and end apart: 11 -> 10, of which waited for: 4 -> 3; matrix products, arithmetic and copies ran while one was open for 8% -> 8% of each run, Pallas kernels for 5% -> 5%
where the time goes in v4:
time: 126 us
  starting transfers between devices  43.8 us (35%)
  blocking collectives  42.5 us (34%)
  Pallas kernels  14.2 us (11%)
  waiting for transfers between devices  12.7 us (10%)
  matrix products  6.41 us (5%)
  local copies, waits for them, and re-layouts  4.53 us (4%)
  between operations  1.48 us (1%)
    all_to_all x2, blocking collectives, swap(): return lax.all_to_all(x, axis, split_axis=0, concat_axis=0, tiled=True)  42.5 us
    ppermute x8, starting transfers between devices, shift(): return lax.ppermute(x, axis, [(s, (s + step) % n) for s in range(n)])  31.5 us
    all_to_all x2, starting transfers between devices, swap(): return lax.all_to_all(x, axis, split_axis=0, concat_axis=0, tiled=True)  12.2 us
    pallas_call x5, Pallas kernels, kernel_call(): pl.pallas_call(body, out_shape=outs, in_specs=specs, out_specs=out_specs,...  12.1 us
    ppermute x8, waiting for transfers between devices, shift(): return lax.ppermute(x, axis, [(s, (s + step) % n) for s in range(n)])  8.4 us
    dot_general x2, matrix products, dot(): lax.dot_general(a, b, (((ca,), (cb,)), ((), ())), precision=PRECISE, pref...  6.41 us
    all_to_all x2, waiting for transfers between devices, swap(): return lax.all_to_all(x, axis, split_axis=0, concat_axis=0, tiled=True)  4.34 us
    unnamed x12, local copies, waits for them, and re-layouts  2.73 us
  transfers between devices with their start and end apart: 10, of which 3 were waited for; matrix products, arithmetic and copies ran while one was open for 8% of the time, Pallas kernels for 5%

profile of v4, /device:TPU:1, one launch (start us, length us, event | category | flops | bytes accessed | tf_op | source)
XLA Modules:
  0.0 125.6 jit_solution(12592105435965984910)
XLA Ops:
  0.6 2.0 %pack.1 = (f32[192,512]{1,0:T(8,128)}, f32[192,512]{1,0:T(8,128)}) custom-call(f32[64,512]{1,0:T(8,128)} %bitcast.28, f32[128,512]{1,0:T(8,128)} %bitcast.26, f32[128,512]{1,0:T(8,128)} %bitcast.27, f32[64,512]{1,0:T(8,128)} %bitcast.29), custom_call_target="tpu_custom_call" | custom-call | tf_op jit(solution)/shard_map/pack/pallas_call | solution.py:199
  2.7 0.0 copy-start.3
  2.7 4.1 %collective-permute-start = (f32[192,512]{1,0:T(8,128)}, f32[192,512]{1,0:T(8,128)S(1)}, u32[]{:S(2)}, u32[]{:S(2)}) collective-permute-start(f32[192,512]{1,0:T(8,128)} %get-tuple-element.13), channel_id=1, source_target_pairs={{0,2},{2,4},{4,6},{6,0},{1,3},{3,5},{5,7},{7,1},{8,10},{10,12},{12... | collective-permute-start | bytes 1179656 | tf_op jit(solution)/shard_map/ppermute | solution.py:27
  6.8 3.2 %collective-permute-start.1 = (f32[192,512]{1,0:T(8,128)}, f32[192,512]{1,0:T(8,128)S(1)}, u32[]{:S(2)}, u32[]{:S(2)}) collective-permute-start(f32[192,512]{1,0:T(8,128)} %get-tuple-element.13), channel_id=1, source_target_pairs={{0,6},{2,0},{4,2},{6,4},{1,7},{3,1},{5,3},{7,5},{8,14},{10,8},{12,... | collective-permute-start | bytes 1179656 | tf_op jit(solution)/shard_map/ppermute | solution.py:27
  10.0 3.6 %collective-permute-start.2 = (f32[192,512]{1,0:T(8,128)}, f32[192,512]{1,0:T(8,128)S(1)}, u32[]{:S(2)}, u32[]{:S(2)}) collective-permute-start(f32[192,512]{1,0:T(8,128)} %get-tuple-element.13), channel_id=1, source_target_pairs={{0,4},{2,6},{4,0},{6,2},{1,5},{3,7},{5,1},{7,3},{8,12},{10,14},{12... | collective-permute-start | bytes 1179656 | tf_op jit(solution)/shard_map/ppermute | solution.py:27
  13.6 1.0 constant_dynamic-update-slice_fusion.3
  14.6 0.0 collective-permute-done
  14.7 0.8 collective-permute-done.1
  15.5 7.6 %collective-permute-done.2 = f32[192,512]{1,0:T(8,128)S(1)} collective-permute-done((f32[192,512]{1,0:T(8,128)}, f32[192,512]{1,0:T(8,128)S(1)}, u32[]{:S(2)}, u32[]{:S(2)}) %collective-permute-start.2) | collective-permute-done | bytes 393248 | tf_op jit(solution)/shard_map/ppermute | solution.py:27
  23.1 8.1 %collective-permute-start.3 = (f32[768,512]{1,0:T(8,128)S(1)}, f32[768,512]{1,0:T(8,128)S(1)}, u32[]{:S(2)}, u32[]{:S(2)}) collective-permute-start(f32[768,512]{1,0:T(8,128)S(1)} %constant_dynamic-update-slice_fusion.mine), channel_id=1, source_target_pairs={{0,1},{1,0},{2,3},{3,2},{4,5},{5,4},{6,7},{7,6},{8,9},{9,8},{10,11... | collective-permute-start | bytes 4718600 | tf_op jit(solution)/shard_map/ppermute | solution.py:27
  31.2 0.0 copy-done.3
  31.2 1.9 %collective-permute-start.4 = (f32[192,512]{1,0:T(8,128)S(1)}, f32[192,512]{1,0:T(8,128)}, u32[]{:S(2)}, u32[]{:S(2)}) collective-permute-start(f32[192,512]{1,0:T(8,128)S(1)} %copy-done.3), channel_id=1, source_target_pairs={{0,1},{1,0},{2,3},{3,2},{4,5},{5,4},{6,7},{7,6},{8,9},{9,8},{10,11... | collective-permute-start | bytes 1179656 | tf_op jit(solution)/shard_map/ppermute | solution.py:27
  33.8 3.7 %shard_map.121 = (f32[256,512]{1,0:T(8,128)}, f32[8,32,640]{2,1,0:T(8,128)}) custom-call(s32[1]{0:T(128)} %bitcast.me, s32[1]{0:T(128)} %bitcast.21.present, f32[512,512]{1,0:T(8,128)} %bitcast.23, f32[512,512]{1,0:T(8,128)} %bitcast.24, f32[512,256]{1,0:T(8,128)} %bitcast.25, f32[64,256]{1,0:T(8,128)} %bitcast.30, f32[2,64,256]{2,1,0:T(8,128)} %rt.1), custom_call_target="tpu_custom_call" | custom-call | tf_op jit(solution)/shard_map/pallas_call | solution.py:38
  37.5 5.0 %all-to-all-start = ((f32[8,32,640]{2,1,0:T(8,128)}), f32[8,32,640]{2,1,0:T(8,128)}, u32[]{:S(2)}, u32[]{:S(2)}) async-start(f32[8,32,640]{2,1,0:T(8,128)} %get-tuple-element.12), calls=%async_computation | async-start | bytes 1310720 | tf_op jit(solution)/shard_map/all_to_all | solution.py:22
  42.5 0.8 constant_dynamic-update-slice_fusion.5
  43.3 0.0 collective-permute-done.4
  43.3 1.8 %constant_dynamic-update-slice_fusion.4.t0 = f32[384,512]{1,0:T(8,128)} fusion(f32[384,512]{1,0:T(8,128)} %constant_dynamic-update-slice_fusion.5, f32[192,512]{1,0:T(8,128)} %collective-permute-done.4), kind=kLoop, calls=%fused_computation.5 | loop fusion | bytes 786432 | tf_op jit(solution)/shard_map/concatenate | solution.py:208
  45.0 3.2 %collective-permute-start.5 = (f32[384,512]{1,0:T(8,128)}, f32[384,512]{1,0:T(8,128)}, u32[]{:S(2)}, u32[]{:S(2)}) collective-permute-start(f32[384,512]{1,0:T(8,128)} %constant_dynamic-update-slice_fusion.4.t0), channel_id=1, source_target_pairs={{0,2},{2,4},{4,6},{6,0},{1,3},{3,5},{5,7},{7,1},{8,10},{10,12},{12... | collective-permute-start | bytes 2359304 | tf_op jit(solution)/shard_map/ppermute | solution.py:27
  48.3 4.3 %collective-permute-start.6 = (f32[384,512]{1,0:T(8,128)}, f32[384,512]{1,0:T(8,128)}, u32[]{:S(2)}, u32[]{:S(2)}) collective-permute-start(f32[384,512]{1,0:T(8,128)} %constant_dynamic-update-slice_fusion.4.t0), channel_id=1, source_target_pairs={{0,4},{2,6},{4,0},{6,2},{1,5},{3,7},{5,1},{7,3},{8,12},{10,14},{12... | collective-permute-start | bytes 2359304 | tf_op jit(solution)/shard_map/ppermute | solution.py:27
  52.6 3.1 %collective-permute-start.7 = (f32[384,512]{1,0:T(8,128)}, f32[384,512]{1,0:T(8,128)}, u32[]{:S(2)}, u32[]{:S(2)}) collective-permute-start(f32[384,512]{1,0:T(8,128)} %constant_dynamic-update-slice_fusion.4.t0), channel_id=1, source_target_pairs={{0,6},{2,0},{4,2},{6,4},{1,7},{3,1},{5,3},{7,5},{8,14},{10,8},{12,... | collective-permute-start | bytes 2359304 | tf_op jit(solution)/shard_map/ppermute | solution.py:27
  55.7 0.0 all-to-all-done.got
  55.7 0.0 collective-permute-done.3.other
  55.7 2.0 %shard_map.122 = (f32[64,4,128]{2,1,0:T(4,128)S(1)}, f32[32,512]{1,0:T(8,128)S(1)}) custom-call(f32[8,32,640]{2,1,0:T(8,128)} %all-to-all-done.got, f32[768,512]{1,0:T(8,128)S(1)} %constant_dynamic-update-slice_fusion.mine, f32[768,512]{1,0:T(8,128)S(1)} %collective-permute-done.3.other), custom_call_target="tpu_custom_call" | custom-call | tf_op jit(solution)/shard_map/pallas_call | solution.py:38
  57.7 27.0 %all_to_all.20.pieces = f32[64,4,128]{2,1,0:T(4,128)S(1)} all-to-all(f32[64,4,128]{2,1,0:T(4,128)S(1)} %get-tuple-element.14), channel_id=1, replica_groups=mesh['leaf'=8,'grow'=8,'gcol_0'=4,'gcol_1'=2] {'leaf','grow'}, dimensions={0} | all-to-all | bytes 262144 | tf_op jit(solution)/shard_map/all_to_all | solution.py:22
  84.7 0.1 shard_map.123
  84.8 15.5 %all_to_all.21.total = f32[64,4,128]{2,1,0:T(4,128)S(1)} all-to-all(f32[64,4,128]{2,1,0:T(4,128)S(1)} %shard_map.123), channel_id=1, replica_groups=mesh['leaf'=8,'grow'=8,'gcol_0'=4,'gcol_1'=2] {'leaf','grow'}, dimensions={0} | all-to-all | bytes 262144 | tf_op jit(solution)/shard_map/all_to_all | solution.py:22
  100.3 0.0 collective-permute-done.5.t1
  100.3 0.0 collective-permute-done.6.t2
  100.3 0.0 collective-permute-done.7.t3
  100.3 4.9 %shard_map.124 = f32[8,32,640]{2,1,0:T(8,128)S(1)} custom-call(f32[1,1,128]{2,1,0:T(1,128)S(1)} %slice.4.late, f32[8,32,640]{2,1,0:T(8,128)} %all-to-all-done.got, f32[64,4,128]{2,1,0:T(4,128)S(1)} %all_to_all.21.total, f32[32,512]{1,0:T(8,128)S(1)} %get-tuple-element.15.mf, f32[384,512]{1,0:T(8,128)} %constant_dynamic-update-slice_fusion.4.t0, ...), custom_call_target="tpu_custom_call" | custom-call | tf_op jit(solution)/shard_map/pallas_call | solution.py:38
  105.2 0.0 copy-start
  105.2 0.8 copy-done
  106.1 0.0 copy-start.1
  106.1 7.3 %all-to-all-start.3 = ((f32[8,32,640]{2,1,0:T(8,128)}), f32[8,32,640]{2,1,0:T(8,128)S(1)}, u32[]{:S(2)}, u32[]{:S(2)}) async-start(f32[8,32,640]{2,1,0:T(8,128)} %copy-done), calls=%async_computation.3 | async-start | bytes 1310720 | tf_op jit(solution)/shard_map/all_to_all | solution.py:22
  113.3 0.0 copy-start.2
  113.3 0.0 copy-done.1
  113.3 2.9 %convolution_bitcast_fusion.lead = f32[512,256]{1,0:T(8,128)S(1)} fusion(f32[256,512]{1,0:T(8,128)} %get-tuple-element.17, f32[1,1,1,512,512]{4,3,2,1,0:T(8,128)S(1)} %copy-done.1), kind=kOutput, calls=%fused_computation | convolution fusion | flops 805306368 | bytes 2097152 | tf_op jit(solution)/shard_map/dot_general | solution.py:16
  116.3 0.0 copy-done.2
  116.3 3.5 %fusion.link = f32[512,512]{1,0:T(8,128)S(1)} fusion(f32[1,1,1,512,512]{4,3,2,1,0:T(8,128)S(1)} %copy-done.2, f32[1,1,1,512,512]{4,3,2,1,0:T(8,128)S(1)} %copy-done.1), kind=kOutput, calls=%fused_computation.7 | convolution fusion | flops 1610612736 | bytes 3145728 | tf_op jit(solution)/shard_map/dot_general | solution.py:16
  119.8 4.3 %all-to-all-done.3.back = f32[8,32,640]{2,1,0:T(8,128)S(1)} async-done(((f32[8,32,640]{2,1,0:T(8,128)}), f32[8,32,640]{2,1,0:T(8,128)S(1)}, u32[]{:S(2)}, u32[]{:S(2)}) %all-to-all-start.3) | async-done | bytes 655392 | tf_op jit(solution)/shard_map/all_to_all | solution.py:22
  124.1 1.5 %shard_map.125 = (f32[512,256]{1,0:T(8,128)}, f32[64,256]{1,0:T(8,128)}, f32[2,64,256]{2,1,0:T(8,128)}) custom-call(s32[1]{0:T(128)} %bitcast.me, s32[1]{0:T(128)} %bitcast.22.present, f32[8,32,640]{2,1,0:T(8,128)S(1)} %all-to-all-done.3.back, f32[512,512]{1,0:T(8,128)S(1)} %fusion.link, f32[512,256]{1,0:T(8,128)S(1)} %convolution_bitcast_fusion.lead), custom_call_target="tpu_custom_call" | custom-call | tf_op jit(solution)/shard_map/pallas_call | solution.py:38
  (4 shorter events, 0.1 us)
Async XLA Ops:
  2.7 28.5 %copy-start.3 = (f32[192,512]{1,0:T(8,128)S(1)}, f32[192,512]{1,0:T(8,128)}, u32[]{:S(2)}) copy-start(f32[192,512]{1,0:T(8,128)} %get-tuple-element.16) | copy-start | bytes 1179652
  2.7 11.9 %collective-permute-start = (f32[192,512]{1,0:T(8,128)}, f32[192,512]{1,0:T(8,128)S(1)}, u32[]{:S(2)}, u32[]{:S(2)}) collective-permute-start(f32[192,512]{1,0:T(8,128)} %get-tuple-element.13), channel_id=1, source_target_pairs={{0,2},{2,4},{4,6},{6,0},{1,3},{3,5},{5,7},{7,1},{8,10},{10,12},{12... | collective-permute-start | bytes 1179656 | tf_op jit(solution)/shard_map/ppermute | solution.py:27
  6.8 8.7 %collective-permute-start.1 = (f32[192,512]{1,0:T(8,128)}, f32[192,512]{1,0:T(8,128)S(1)}, u32[]{:S(2)}, u32[]{:S(2)}) collective-permute-start(f32[192,512]{1,0:T(8,128)} %get-tuple-element.13), channel_id=1, source_target_pairs={{0,6},{2,0},{4,2},{6,4},{1,7},{3,1},{5,3},{7,5},{8,14},{10,8},{12,... | collective-permute-start | bytes 1179656 | tf_op jit(solution)/shard_map/ppermute | solution.py:27
  10.0 13.1 %collective-permute-start.2 = (f32[192,512]{1,0:T(8,128)}, f32[192,512]{1,0:T(8,128)S(1)}, u32[]{:S(2)}, u32[]{:S(2)}) collective-permute-start(f32[192,512]{1,0:T(8,128)} %get-tuple-element.13), channel_id=1, source_target_pairs={{0,4},{2,6},{4,0},{6,2},{1,5},{3,7},{5,1},{7,3},{8,12},{10,14},{12... | collective-permute-start | bytes 1179656 | tf_op jit(solution)/shard_map/ppermute | solution.py:27
  23.1 32.6 %collective-permute-start.3 = (f32[768,512]{1,0:T(8,128)S(1)}, f32[768,512]{1,0:T(8,128)S(1)}, u32[]{:S(2)}, u32[]{:S(2)}) collective-permute-start(f32[768,512]{1,0:T(8,128)S(1)} %constant_dynamic-update-slice_fusion.mine), channel_id=1, source_target_pairs={{0,1},{1,0},{2,3},{3,2},{4,5},{5,4},{6,7},{7,6},{8,9},{9,8},{10,11... | collective-permute-start | bytes 4718600 | tf_op jit(solution)/shard_map/ppermute | solution.py:27
  31.2 12.0 %collective-permute-start.4 = (f32[192,512]{1,0:T(8,128)S(1)}, f32[192,512]{1,0:T(8,128)}, u32[]{:S(2)}, u32[]{:S(2)}) collective-permute-start(f32[192,512]{1,0:T(8,128)S(1)} %copy-done.3), channel_id=1, source_target_pairs={{0,1},{1,0},{2,3},{3,2},{4,5},{5,4},{6,7},{7,6},{8,9},{9,8},{10,11... | collective-permute-start | bytes 1179656 | tf_op jit(solution)/shard_map/ppermute | solution.py:27
  37.5 18.2 %all-to-all-start = ((f32[8,32,640]{2,1,0:T(8,128)}), f32[8,32,640]{2,1,0:T(8,128)}, u32[]{:S(2)}, u32[]{:S(2)}) async-start(f32[8,32,640]{2,1,0:T(8,128)} %get-tuple-element.12), calls=%async_computation | async-start | bytes 1310720 | tf_op jit(solution)/shard_map/all_to_all | solution.py:22
  45.0 55.2 %collective-permute-start.5 = (f32[384,512]{1,0:T(8,128)}, f32[384,512]{1,0:T(8,128)}, u32[]{:S(2)}, u32[]{:S(2)}) collective-permute-start(f32[384,512]{1,0:T(8,128)} %constant_dynamic-update-slice_fusion.4.t0), channel_id=1, source_target_pairs={{0,2},{2,4},{4,6},{6,0},{1,3},{3,5},{5,7},{7,1},{8,10},{10,12},{12... | collective-permute-start | bytes 2359304 | tf_op jit(solution)/shard_map/ppermute | solution.py:27
  48.3 52.0 %collective-permute-start.6 = (f32[384,512]{1,0:T(8,128)}, f32[384,512]{1,0:T(8,128)}, u32[]{:S(2)}, u32[]{:S(2)}) collective-permute-start(f32[384,512]{1,0:T(8,128)} %constant_dynamic-update-slice_fusion.4.t0), channel_id=1, source_target_pairs={{0,4},{2,6},{4,0},{6,2},{1,5},{3,7},{5,1},{7,3},{8,12},{10,14},{12... | collective-permute-start | bytes 2359304 | tf_op jit(solution)/shard_map/ppermute | solution.py:27
  52.6 47.7 %collective-permute-start.7 = (f32[384,512]{1,0:T(8,128)}, f32[384,512]{1,0:T(8,128)}, u32[]{:S(2)}, u32[]{:S(2)}) collective-permute-start(f32[384,512]{1,0:T(8,128)} %constant_dynamic-update-slice_fusion.4.t0), channel_id=1, source_target_pairs={{0,6},{2,0},{4,2},{6,4},{1,7},{3,1},{5,3},{7,5},{8,14},{10,8},{12,... | collective-permute-start | bytes 2359304 | tf_op jit(solution)/shard_map/ppermute | solution.py:27
  105.2 0.9 copy-start
  106.1 7.3 %copy-start.1 = (f32[1,1,1,512,512]{4,3,2,1,0:T(8,128)S(1)}, f32[1,1,1,512,512]{4,3,2,1,0:T(8,128)}, u32[]{:S(2)}) copy-start(f32[1,1,1,512,512]{4,3,2,1,0:T(8,128)} %param.11) | copy-start | bytes 3145732
  106.1 18.0 %all-to-all-start.3 = ((f32[8,32,640]{2,1,0:T(8,128)}), f32[8,32,640]{2,1,0:T(8,128)S(1)}, u32[]{:S(2)}, u32[]{:S(2)}) async-start(f32[8,32,640]{2,1,0:T(8,128)} %copy-done), calls=%async_computation.3 | async-start | bytes 1310720 | tf_op jit(solution)/shard_map/all_to_all | solution.py:22
  113.3 3.0 %copy-start.2 = (f32[1,1,1,512,512]{4,3,2,1,0:T(8,128)S(1)}, f32[1,1,1,512,512]{4,3,2,1,0:T(8,128)}, u32[]{:S(2)}) copy-start(f32[1,1,1,512,512]{4,3,2,1,0:T(8,128)} %param.12) | copy-start | bytes 3145732

commit v5 on v4

--- a/solution.py
+++ b/solution.py
@@ -31,9 +31,9 @@
     return jax.ShapeDtypeStruct(shape, jnp.float32)
 
 
-def kernel_call(body, outs, *args, scalars=0, scratch=(), limit=24):
+def kernel_call(body, outs, *args, scalars=0, scratch=(), limit=24, space=pltpu.VMEM):
     specs = [pl.BlockSpec(memory_space=pltpu.SMEM)] * scalars
-    specs += [pl.BlockSpec(memory_space=pltpu.VMEM)] * (len(args) - scalars)
+    specs += [pl.BlockSpec(memory_space=space)] * (len(args) - scalars)
     out_specs = jax.tree.map(lambda _: pl.BlockSpec(memory_space=pltpu.VMEM), outs)
     return pl.pallas_call(
         body, out_shape=outs, in_specs=specs, out_specs=out_specs, scratch_shapes=scratch,
@@ -72,13 +72,21 @@
         c.wait()
 
 
-def leaf_kernel(me, present, il, ll, rl, rm, rt, lead_in, sent):
+def leaf_kernel(me, present, il_far, ll_far, rl_far, rm_far, rt_far, lead_in, sent, il, ll, rl, rm, rt, sems):
+    pairs = [(rl_far, rl), (il_far, il), (ll_far, ll), (rm_far, rm), (rt_far, rt)]
+    copies = [pltpu.make_async_copy(a, b, sems.at[i]) for i, (a, b) in enumerate(pairs)]
+    for c in copies:
+        c.start()
     n_g, cols, _ = sent.shape
     block = il.shape[0]
     share = block // n_g
     kept = present[0].astype(jnp.float32)
+    copies[0].wait()
+    copies[1].wait()
     fwd = dot3(split(rl[...].T), split(il[...]), 1, 1)
     lead_in[...] = fwd
+    for c in copies[2:]:
+        c.wait()
     part = dot3(split(fwd), split(ll[...]), 1, 1) * kept
     lane = lax.broadcasted_iota(jnp.int32, (1, block), 1)
     own = (lane >= me[0] * share) & (lane < (me[0] + 1) * share)
@@ -210,7 +218,11 @@
         leaf_kernel,
         (f32(nrhs, block), f32(n_g, cols, block + 2 * share)),
         me.reshape(1).astype(jnp.int32), present.reshape(1), il, ll, rl, right_middle[0, 0], right_top,
-        scalars=2, limit=None,
+        scalars=2, limit=None, space=pl.ANY,
+        scratch=[
+            *(pltpu.VMEM(a.shape, jnp.float32) for a in (il, ll, rl, right_middle[0, 0], right_top)),
+            pltpu.SemaphoreType.DMA((5,)),
+        ],
     )
     lead = dot(il, leaf_fwd, 0, 1)
     link = dot(il, ll, 0, 1)

time: 126 us -> 126 us (level)
  transfers between devices with their start and end apart: 10 -> 10, of which waited for: 3 -> 3; matrix products, arithmetic and copies ran while one was open for 8% -> 8% of each run, Pallas kernels for 5% -> 4%
where the time goes in v5:
time: 126 us; the launch traced here: 125 us
  starting transfers between devices  43.8 us (35%)
  blocking collectives  42.5 us (34%)
  Pallas kernels  14 us (11%)
  waiting for transfers between devices  12.7 us (10%)
  matrix products  6.41 us (5%)
  local copies, waits for them, and re-layouts  4.53 us (4%)
  between operations  1.49 us (1%)
    all_to_all x2, blocking collectives, swap(): return lax.all_to_all(x, axis, split_axis=0, concat_axis=0, tiled=True)  42.5 us
    ppermute x8, starting transfers between devices, shift(): return lax.ppermute(x, axis, [(s, (s + step) % n) for s in range(n)])  31.5 us
    all_to_all x2, starting transfers between devices, swap(): return lax.all_to_all(x, axis, split_axis=0, concat_axis=0, tiled=True)  12.3 us
    pallas_call x5, Pallas kernels, kernel_call(): pl.pallas_call(body, out_shape=outs, in_specs=specs, out_specs=out_specs,...  11.9 us
    ppermute x8, waiting for transfers between devices, shift(): return lax.ppermute(x, axis, [(s, (s + step) % n) for s in range(n)])  8.4 us
    dot_general x2, matrix products, dot(): lax.dot_general(a, b, (((ca,), (cb,)), ((), ())), precision=PRECISE, pref...  6.41 us
    all_to_all x2, waiting for transfers between devices, swap(): return lax.all_to_all(x, axis, split_axis=0, concat_axis=0, tiled=True)  4.34 us
    unnamed x12, local copies, waits for them, and re-layouts  2.73 us
  transfers between devices with their start and end apart: 10, of which 3 were waited for; matrix products, arithmetic and copies ran while one was open for 8% of the time, Pallas kernels for 4%

profile of v5, /device:TPU:1, one launch (start us, length us, event | category | flops | bytes accessed | tf_op | source)
XLA Modules:
  0.0 125.4 jit_solution(17113780479179683745)
XLA Ops:
  0.6 2.0 %pack.1 = (f32[192,512]{1,0:T(8,128)}, f32[192,512]{1,0:T(8,128)}) custom-call(f32[64,512]{1,0:T(8,128)} %bitcast.28, f32[128,512]{1,0:T(8,128)} %bitcast.26, f32[128,512]{1,0:T(8,128)} %bitcast.27, f32[64,512]{1,0:T(8,128)} %bitcast.29), custom_call_target="tpu_custom_call" | custom-call | tf_op jit(solution)/shard_map/pack/pallas_call | solution.py:207
  2.7 0.0 copy-start.3
  2.7 4.1 %collective-permute-start = (f32[192,512]{1,0:T(8,128)}, f32[192,512]{1,0:T(8,128)S(1)}, u32[]{:S(2)}, u32[]{:S(2)}) collective-permute-start(f32[192,512]{1,0:T(8,128)} %get-tuple-element.13), channel_id=1, source_target_pairs={{0,2},{2,4},{4,6},{6,0},{1,3},{3,5},{5,7},{7,1},{8,10},{10,12},{12... | collective-permute-start | bytes 1179656 | tf_op jit(solution)/shard_map/ppermute | solution.py:27
  6.8 3.2 %collective-permute-start.1 = (f32[192,512]{1,0:T(8,128)}, f32[192,512]{1,0:T(8,128)S(1)}, u32[]{:S(2)}, u32[]{:S(2)}) collective-permute-start(f32[192,512]{1,0:T(8,128)} %get-tuple-element.13), channel_id=1, source_target_pairs={{0,6},{2,0},{4,2},{6,4},{1,7},{3,1},{5,3},{7,5},{8,14},{10,8},{12,... | collective-permute-start | bytes 1179656 | tf_op jit(solution)/shard_map/ppermute | solution.py:27
  10.0 3.6 %collective-permute-start.2 = (f32[192,512]{1,0:T(8,128)}, f32[192,512]{1,0:T(8,128)S(1)}, u32[]{:S(2)}, u32[]{:S(2)}) collective-permute-start(f32[192,512]{1,0:T(8,128)} %get-tuple-element.13), channel_id=1, source_target_pairs={{0,4},{2,6},{4,0},{6,2},{1,5},{3,7},{5,1},{7,3},{8,12},{10,14},{12... | collective-permute-start | bytes 1179656 | tf_op jit(solution)/shard_map/ppermute | solution.py:27
  13.6 1.0 constant_dynamic-update-slice_fusion.3
  14.6 0.0 collective-permute-done
  14.7 0.8 collective-permute-done.1
  15.5 7.6 %collective-permute-done.2 = f32[192,512]{1,0:T(8,128)S(1)} collective-permute-done((f32[192,512]{1,0:T(8,128)}, f32[192,512]{1,0:T(8,128)S(1)}, u32[]{:S(2)}, u32[]{:S(2)}) %collective-permute-start.2) | collective-permute-done | bytes 393248 | tf_op jit(solution)/shard_map/ppermute | solution.py:27
  23.1 8.1 %collective-permute-start.3 = (f32[768,512]{1,0:T(8,128)S(1)}, f32[768,512]{1,0:T(8,128)S(1)}, u32[]{:S(2)}, u32[]{:S(2)}) collective-permute-start(f32[768,512]{1,0:T(8,128)S(1)} %constant_dynamic-update-slice_fusion.mine), channel_id=1, source_target_pairs={{0,1},{1,0},{2,3},{3,2},{4,5},{5,4},{6,7},{7,6},{8,9},{9,8},{10,11... | collective-permute-start | bytes 4718600 | tf_op jit(solution)/shard_map/ppermute | solution.py:27
  31.2 0.0 copy-done.3
  31.2 1.9 %collective-permute-start.4 = (f32[192,512]{1,0:T(8,128)S(1)}, f32[192,512]{1,0:T(8,128)}, u32[]{:S(2)}, u32[]{:S(2)}) collective-permute-start(f32[192,512]{1,0:T(8,128)S(1)} %copy-done.3), channel_id=1, source_target_pairs={{0,1},{1,0},{2,3},{3,2},{4,5},{5,4},{6,7},{7,6},{8,9},{9,8},{10,11... | collective-permute-start | bytes 1179656 | tf_op jit(solution)/shard_map/ppermute | solution.py:27
  33.8 3.5 %shard_map.121 = (f32[256,512]{1,0:T(8,128)}, f32[8,32,640]{2,1,0:T(8,128)}) custom-call(s32[1]{0:T(128)} %bitcast.me, s32[1]{0:T(128)} %bitcast.21.present, f32[512,512]{1,0:T(8,128)} %bitcast.23, f32[512,512]{1,0:T(8,128)} %bitcast.24, f32[512,256]{1,0:T(8,128)} %bitcast.25, f32[64,256]{1,0:T(8,128)} %bitcast.30, f32[2,64,256]{2,1,0:T(8,128)} %rt_far.1), custom_call_target="tpu_custom_call" | custom-call | tf_op jit(solution)/shard_map/pallas_call | solution.py:38
  37.3 5.0 %all-to-all-start = ((f32[8,32,640]{2,1,0:T(8,128)}), f32[8,32,640]{2,1,0:T(8,128)}, u32[]{:S(2)}, u32[]{:S(2)}) async-start(f32[8,32,640]{2,1,0:T(8,128)} %get-tuple-element.12), calls=%async_computation | async-start | bytes 1310720 | tf_op jit(solution)/shard_map/all_to_all | solution.py:22
  42.3 0.8 constant_dynamic-update-slice_fusion.5
  43.1 0.0 collective-permute-done.4
  43.1 1.8 %constant_dynamic-update-slice_fusion.4.t0 = f32[384,512]{1,0:T(8,128)} fusion(f32[384,512]{1,0:T(8,128)} %constant_dynamic-update-slice_fusion.5, f32[192,512]{1,0:T(8,128)} %collective-permute-done.4), kind=kLoop, calls=%fused_computation.5 | loop fusion | bytes 786432 | tf_op jit(solution)/shard_map/concatenate | solution.py:216
  44.9 3.2 %collective-permute-start.5 = (f32[384,512]{1,0:T(8,128)}, f32[384,512]{1,0:T(8,128)}, u32[]{:S(2)}, u32[]{:S(2)}) collective-permute-start(f32[384,512]{1,0:T(8,128)} %constant_dynamic-update-slice_fusion.4.t0), channel_id=1, source_target_pairs={{0,2},{2,4},{4,6},{6,0},{1,3},{3,5},{5,7},{7,1},{8,10},{10,12},{12... | collective-permute-start | bytes 2359304 | tf_op jit(solution)/shard_map/ppermute | solution.py:27
  48.1 4.3 %collective-permute-start.6 = (f32[384,512]{1,0:T(8,128)}, f32[384,512]{1,0:T(8,128)}, u32[]{:S(2)}, u32[]{:S(2)}) collective-permute-start(f32[384,512]{1,0:T(8,128)} %constant_dynamic-update-slice_fusion.4.t0), channel_id=1, source_target_pairs={{0,4},{2,6},{4,0},{6,2},{1,5},{3,7},{5,1},{7,3},{8,12},{10,14},{12... | collective-permute-start | bytes 2359304 | tf_op jit(solution)/shard_map/ppermute | solution.py:27
  52.5 3.1 %collective-permute-start.7 = (f32[384,512]{1,0:T(8,128)}, f32[384,512]{1,0:T(8,128)}, u32[]{:S(2)}, u32[]{:S(2)}) collective-permute-start(f32[384,512]{1,0:T(8,128)} %constant_dynamic-update-slice_fusion.4.t0), channel_id=1, source_target_pairs={{0,6},{2,0},{4,2},{6,4},{1,7},{3,1},{5,3},{7,5},{8,14},{10,8},{12,... | collective-permute-start | bytes 2359304 | tf_op jit(solution)/shard_map/ppermute | solution.py:27
  55.6 0.0 all-to-all-done.got
  55.6 0.0 collective-permute-done.3.other
  55.6 2.0 %shard_map.122 = (f32[64,4,128]{2,1,0:T(4,128)S(1)}, f32[32,512]{1,0:T(8,128)S(1)}) custom-call(f32[8,32,640]{2,1,0:T(8,128)} %all-to-all-done.got, f32[768,512]{1,0:T(8,128)S(1)} %constant_dynamic-update-slice_fusion.mine, f32[768,512]{1,0:T(8,128)S(1)} %collective-permute-done.3.other), custom_call_target="tpu_custom_call" | custom-call | tf_op jit(solution)/shard_map/pallas_call | solution.py:38
  57.5 27.0 %all_to_all.20.pieces = f32[64,4,128]{2,1,0:T(4,128)S(1)} all-to-all(f32[64,4,128]{2,1,0:T(4,128)S(1)} %get-tuple-element.14), channel_id=1, replica_groups=mesh['leaf'=8,'grow'=8,'gcol_0'=4,'gcol_1'=2] {'leaf','grow'}, dimensions={0} | all-to-all | bytes 262144 | tf_op jit(solution)/shard_map/all_to_all | solution.py:22
  84.5 0.1 shard_map.123
  84.6 15.5 %all_to_all.21.total = f32[64,4,128]{2,1,0:T(4,128)S(1)} all-to-all(f32[64,4,128]{2,1,0:T(4,128)S(1)} %shard_map.123), channel_id=1, replica_groups=mesh['leaf'=8,'grow'=8,'gcol_0'=4,'gcol_1'=2] {'leaf','grow'}, dimensions={0} | all-to-all | bytes 262144 | tf_op jit(solution)/shard_map/all_to_all | solution.py:22
  100.1 0.0 collective-permute-done.5.t1
  100.1 0.0 collective-permute-done.6.t2
  100.1 0.0 collective-permute-done.7.t3
  100.1 4.9 %shard_map.124 = f32[8,32,640]{2,1,0:T(8,128)S(1)} custom-call(f32[1,1,128]{2,1,0:T(1,128)S(1)} %slice.4.late, f32[8,32,640]{2,1,0:T(8,128)} %all-to-all-done.got, f32[64,4,128]{2,1,0:T(4,128)S(1)} %all_to_all.21.total, f32[32,512]{1,0:T(8,128)S(1)} %get-tuple-element.15.mf, f32[384,512]{1,0:T(8,128)} %constant_dynamic-update-slice_fusion.4.t0, ...), custom_call_target="tpu_custom_call" | custom-call | tf_op jit(solution)/shard_map/pallas_call | solution.py:38
  105.0 0.0 copy-start
  105.0 0.8 copy-done
  105.9 0.0 copy-start.1
  105.9 7.3 %all-to-all-start.3 = ((f32[8,32,640]{2,1,0:T(8,128)}), f32[8,32,640]{2,1,0:T(8,128)S(1)}, u32[]{:S(2)}, u32[]{:S(2)}) async-start(f32[8,32,640]{2,1,0:T(8,128)} %copy-done), calls=%async_computation.3 | async-start | bytes 1310720 | tf_op jit(solution)/shard_map/all_to_all | solution.py:22
  113.2 0.0 copy-start.2
  113.2 0.0 copy-done.1
  113.2 2.9 %convolution_bitcast_fusion.lead = f32[512,256]{1,0:T(8,128)S(1)} fusion(f32[256,512]{1,0:T(8,128)} %get-tuple-element.17, f32[1,1,1,512,512]{4,3,2,1,0:T(8,128)S(1)} %copy-done.1), kind=kOutput, calls=%fused_computation | convolution fusion | flops 805306368 | bytes 2097152 | tf_op jit(solution)/shard_map/dot_general | solution.py:16
  116.1 0.0 copy-done.2
  116.1 3.5 %fusion.link = f32[512,512]{1,0:T(8,128)S(1)} fusion(f32[1,1,1,512,512]{4,3,2,1,0:T(8,128)S(1)} %copy-done.2, f32[1,1,1,512,512]{4,3,2,1,0:T(8,128)S(1)} %copy-done.1), kind=kOutput, calls=%fused_computation.7 | convolution fusion | flops 1610612736 | bytes 3145728 | tf_op jit(solution)/shard_map/dot_general | solution.py:16
  119.6 4.3 %all-to-all-done.3.back = f32[8,32,640]{2,1,0:T(8,128)S(1)} async-done(((f32[8,32,640]{2,1,0:T(8,128)}), f32[8,32,640]{2,1,0:T(8,128)S(1)}, u32[]{:S(2)}, u32[]{:S(2)}) %all-to-all-start.3) | async-done | bytes 655392 | tf_op jit(solution)/shard_map/all_to_all | solution.py:22
  124.0 1.5 %shard_map.125 = (f32[512,256]{1,0:T(8,128)}, f32[64,256]{1,0:T(8,128)}, f32[2,64,256]{2,1,0:T(8,128)}) custom-call(s32[1]{0:T(128)} %bitcast.me, s32[1]{0:T(128)} %bitcast.22.present, f32[8,32,640]{2,1,0:T(8,128)S(1)} %all-to-all-done.3.back, f32[512,512]{1,0:T(8,128)S(1)} %fusion.link, f32[512,256]{1,0:T(8,128)S(1)} %convolution_bitcast_fusion.lead), custom_call_target="tpu_custom_call" | custom-call | tf_op jit(solution)/shard_map/pallas_call | solution.py:38
  (4 shorter events, 0.1 us)
Async XLA Ops:
  2.7 28.5 %copy-start.3 = (f32[192,512]{1,0:T(8,128)S(1)}, f32[192,512]{1,0:T(8,128)}, u32[]{:S(2)}) copy-start(f32[192,512]{1,0:T(8,128)} %get-tuple-element.16) | copy-start | bytes 1179652
  2.7 11.9 %collective-permute-start = (f32[192,512]{1,0:T(8,128)}, f32[192,512]{1,0:T(8,128)S(1)}, u32[]{:S(2)}, u32[]{:S(2)}) collective-permute-start(f32[192,512]{1,0:T(8,128)} %get-tuple-element.13), channel_id=1, source_target_pairs={{0,2},{2,4},{4,6},{6,0},{1,3},{3,5},{5,7},{7,1},{8,10},{10,12},{12... | collective-permute-start | bytes 1179656 | tf_op jit(solution)/shard_map/ppermute | solution.py:27
  6.8 8.7 %collective-permute-start.1 = (f32[192,512]{1,0:T(8,128)}, f32[192,512]{1,0:T(8,128)S(1)}, u32[]{:S(2)}, u32[]{:S(2)}) collective-permute-start(f32[192,512]{1,0:T(8,128)} %get-tuple-element.13), channel_id=1, source_target_pairs={{0,6},{2,0},{4,2},{6,4},{1,7},{3,1},{5,3},{7,5},{8,14},{10,8},{12,... | collective-permute-start | bytes 1179656 | tf_op jit(solution)/shard_map/ppermute | solution.py:27
  10.0 13.1 %collective-permute-start.2 = (f32[192,512]{1,0:T(8,128)}, f32[192,512]{1,0:T(8,128)S(1)}, u32[]{:S(2)}, u32[]{:S(2)}) collective-permute-start(f32[192,512]{1,0:T(8,128)} %get-tuple-element.13), channel_id=1, source_target_pairs={{0,4},{2,6},{4,0},{6,2},{1,5},{3,7},{5,1},{7,3},{8,12},{10,14},{12... | collective-permute-start | bytes 1179656 | tf_op jit(solution)/shard_map/ppermute | solution.py:27
  23.1 32.4 %collective-permute-start.3 = (f32[768,512]{1,0:T(8,128)S(1)}, f32[768,512]{1,0:T(8,128)S(1)}, u32[]{:S(2)}, u32[]{:S(2)}) collective-permute-start(f32[768,512]{1,0:T(8,128)S(1)} %constant_dynamic-update-slice_fusion.mine), channel_id=1, source_target_pairs={{0,1},{1,0},{2,3},{3,2},{4,5},{5,4},{6,7},{7,6},{8,9},{9,8},{10,11... | collective-permute-start | bytes 4718600 | tf_op jit(solution)/shard_map/ppermute | solution.py:27
  31.2 11.9 %collective-permute-start.4 = (f32[192,512]{1,0:T(8,128)S(1)}, f32[192,512]{1,0:T(8,128)}, u32[]{:S(2)}, u32[]{:S(2)}) collective-permute-start(f32[192,512]{1,0:T(8,128)S(1)} %copy-done.3), channel_id=1, source_target_pairs={{0,1},{1,0},{2,3},{3,2},{4,5},{5,4},{6,7},{7,6},{8,9},{9,8},{10,11... | collective-permute-start | bytes 1179656 | tf_op jit(solution)/shard_map/ppermute | solution.py:27
  37.3 18.2 %all-to-all-start = ((f32[8,32,640]{2,1,0:T(8,128)}), f32[8,32,640]{2,1,0:T(8,128)}, u32[]{:S(2)}, u32[]{:S(2)}) async-start(f32[8,32,640]{2,1,0:T(8,128)} %get-tuple-element.12), calls=%async_computation | async-start | bytes 1310720 | tf_op jit(solution)/shard_map/all_to_all | solution.py:22
  44.9 55.2 %collective-permute-start.5 = (f32[384,512]{1,0:T(8,128)}, f32[384,512]{1,0:T(8,128)}, u32[]{:S(2)}, u32[]{:S(2)}) collective-permute-start(f32[384,512]{1,0:T(8,128)} %constant_dynamic-update-slice_fusion.4.t0), channel_id=1, source_target_pairs={{0,2},{2,4},{4,6},{6,0},{1,3},{3,5},{5,7},{7,1},{8,10},{10,12},{12... | collective-permute-start | bytes 2359304 | tf_op jit(solution)/shard_map/ppermute | solution.py:27
  48.1 52.0 %collective-permute-start.6 = (f32[384,512]{1,0:T(8,128)}, f32[384,512]{1,0:T(8,128)}, u32[]{:S(2)}, u32[]{:S(2)}) collective-permute-start(f32[384,512]{1,0:T(8,128)} %constant_dynamic-update-slice_fusion.4.t0), channel_id=1, source_target_pairs={{0,4},{2,6},{4,0},{6,2},{1,5},{3,7},{5,1},{7,3},{8,12},{10,14},{12... | collective-permute-start | bytes 2359304 | tf_op jit(solution)/shard_map/ppermute | solution.py:27
  52.5 47.7 %collective-permute-start.7 = (f32[384,512]{1,0:T(8,128)}, f32[384,512]{1,0:T(8,128)}, u32[]{:S(2)}, u32[]{:S(2)}) collective-permute-start(f32[384,512]{1,0:T(8,128)} %constant_dynamic-update-slice_fusion.4.t0), channel_id=1, source_target_pairs={{0,6},{2,0},{4,2},{6,4},{1,7},{3,1},{5,3},{7,5},{8,14},{10,8},{12,... | collective-permute-start | bytes 2359304 | tf_op jit(solution)/shard_map/ppermute | solution.py:27
  105.0 0.9 copy-start
  105.9 7.3 %copy-start.1 = (f32[1,1,1,512,512]{4,3,2,1,0:T(8,128)S(1)}, f32[1,1,1,512,512]{4,3,2,1,0:T(8,128)}, u32[]{:S(2)}) copy-start(f32[1,1,1,512,512]{4,3,2,1,0:T(8,128)} %param.11) | copy-start | bytes 3145732
  105.9 18.1 %all-to-all-start.3 = ((f32[8,32,640]{2,1,0:T(8,128)}), f32[8,32,640]{2,1,0:T(8,128)S(1)}, u32[]{:S(2)}, u32[]{:S(2)}) async-start(f32[8,32,640]{2,1,0:T(8,128)} %copy-done), calls=%async_computation.3 | async-start | bytes 1310720 | tf_op jit(solution)/shard_map/all_to_all | solution.py:22
  113.2 3.0 %copy-start.2 = (f32[1,1,1,512,512]{4,3,2,1,0:T(8,128)S(1)}, f32[1,1,1,512,512]{4,3,2,1,0:T(8,128)}, u32[]{:S(2)}) copy-start(f32[1,1,1,512,512]{4,3,2,1,0:T(8,128)} %param.12) | copy-start | bytes 3145732
